TPU v7x, 32 devices: a whole 2x2x4 slice. The times are simulated.
32 devices in a mesh: seq: 8 (over z, x), mp: 4 (over y, core).
Axes of the slice: x: 2, y: 2, z: 4, core: 2. Of those that a mesh axis runs over, the one named last changes fastest.
Arguments:
- patches: bfloat16 [8192, 1280], P('seq'), may hold values from -6 to 6
- clip_of: int32 [8192, 1], P('seq'), may hold values from 0 to 7; in each aligned block of 1024 rows (0 to 1023, 1024 to 2047, ...) at most 256 rows name the same one
- owner_of: int32 [8], replicated, may hold values from 0 to 7, each once
- cites: int32 [256, 4], P('seq'), may hold values from 0 to 7, all different within a row; in each aligned block of 32 rows (0 to 31, 32 to 63, ...) at most 32 rows name the same one
- latent_init: bfloat16 [64, 1280], replicated
- w_query: bfloat16 [1280, 1280], P(None, 'mp'), may hold values from -0.15625 to 0.15625
- w_key: bfloat16 [1280, 1280], P(None, 'mp'), may hold values from -0.15625 to 0.15625
- w_value: bfloat16 [1280, 1280], P(None, 'mp'), may hold values from -0.15625 to 0.15625
- w_out: bfloat16 [1280, 1280], P('mp'), may hold values from -0.15625 to 0.15625
- wx_key: bfloat16 [1280, 4096], P(None, 'mp'), may hold values from -0.15625 to 0.15625
- wx_value: bfloat16 [1280, 4096], P(None, 'mp'), may hold values from -0.15625 to 0.15625
- queries: bfloat16 [4096, 4096], P('seq', 'mp')
Outputs:
- resampled: bfloat16 [512, 1280], P('seq')
- context: bfloat16 [4096, 4096], P('seq', 'mp')
Inputs may be any that keep to these rules, and one draw needn't show every extreme that they name: `clip_of`: within the 1024 patch rows of one index of seq at most 256 name the same clip, and some clip reaches 256. `owner_of`: each index of seq owns exactly one clip. A question cites 4 different clips; among the 32 questions of one index of seq no clip is cited more than 32 times, and some clip reaches 32.
All inputs are finite; a program needn't handle non-finite values.
Results may differ from a plain program's by a relative error of at most 0.023.
The roundings to bfloat16 on the way count: a program that leaves them out, or rounds other values in their place, can miss the bound.
Values may be sent and summed in bfloat16 or wider, within the bound.
No kernel may reach another device: no remote copies, remote signals or barrier semaphores. Data moves between devices by JAX's collectives and lax.ppermute only.
A program may use at most 128 MiB of HBM per device.

v0:
```python
import math

import jax
import jax.numpy as jnp
from jax import lax
from jax.sharding import PartitionSpec as P

RHD = 80
LAT = 64
HD = 128


masked_score = -1e30


def merge_parts(part_out, part_max, part_sum):
    best_max = jnp.max(part_max, axis=1)
    rescale = jnp.exp(part_max - best_max[:, None])
    denominator = jnp.sum(rescale * part_sum, axis=1)
    numerator = jnp.sum(rescale[..., None] * part_out.astype(jnp.float32), axis=1)
    return numerator / denominator[..., None]


def body(
    patches,
    clip_of,
    owner_of,
    cites,
    latent_init,
    w_query,
    w_key,
    w_value,
    w_out,
    wx_key,
    wx_value,
    queries,
):
    groups = lax.axis_size("seq")
    row_count = patches.shape[0]
    slot_count = 2 * row_count // groups
    feature_width = patches.shape[1]
    clip_total = owner_of.shape[0]
    clip_hot = (clip_of == jnp.arange(clip_total, dtype=jnp.int32)[None, :]).astype(jnp.int32)
    target = jnp.sum(clip_hot * owner_of[None, :], axis=1)
    target_hot = (target[:, None] == jnp.arange(groups, dtype=jnp.int32)[None, :]).astype(jnp.int32)
    before = jnp.cumsum(target_hot, axis=0) - target_hot
    placing = target * slot_count + jnp.sum(before * target_hot, axis=1)
    outgoing = (
        jnp.zeros((groups * slot_count, feature_width), jnp.bfloat16).at[placing].set(patches)
    )
    outgoing = outgoing.reshape(groups, slot_count, feature_width)
    live_flags = (
        jnp.zeros((groups * slot_count,), jnp.bfloat16)
        .at[placing]
        .set(1.0)
        .reshape(groups, slot_count)
    )
    arrived, live_slots = (
        lax.all_to_all(outgoing, "seq", split_axis=0, concat_axis=0, tiled=True),
        lax.all_to_all(live_flags, "seq", split_axis=0, concat_axis=0, tiled=True),
    )
    arrived = arrived.reshape(groups * slot_count, feature_width)
    live_slots = live_slots.reshape(groups * slot_count) > 0
    key_rows = jnp.concatenate(
        [
            jnp.dot(arrived, w_key, preferred_element_type=jnp.float32).astype(jnp.bfloat16),
            jnp.dot(latent_init, w_key, preferred_element_type=jnp.float32).astype(jnp.bfloat16),
        ],
        axis=0,
    )
    value_rows = jnp.concatenate(
        [
            jnp.dot(arrived, w_value, preferred_element_type=jnp.float32).astype(jnp.bfloat16),
            jnp.dot(latent_init, w_value, preferred_element_type=jnp.float32).astype(jnp.bfloat16),
        ],
        axis=0,
    )
    latent_query = jnp.dot(latent_init, w_query, preferred_element_type=jnp.float32).astype(
        jnp.bfloat16
    )
    local_heads = latent_query.shape[1] // RHD
    query_heads = latent_query.reshape(LAT, local_heads, RHD)
    key_heads = key_rows.reshape(-1, local_heads, RHD)
    value_heads = value_rows.reshape(-1, local_heads, RHD)
    key_mask = jnp.concatenate([live_slots, jnp.ones((LAT,), jnp.bool_)])
    scores = jnp.einsum(
        "qhd,khd->hqk", query_heads, key_heads, preferred_element_type=jnp.float32
    ) * (1.0 / math.sqrt(RHD))
    scores = jnp.where(key_mask[None, None, :], scores, masked_score)
    row_max = jnp.max(scores, axis=-1)
    raised = jnp.exp(scores - row_max[..., None])
    row_sum = jnp.sum(raised, axis=-1)
    weights = (raised / row_sum[..., None]).astype(jnp.bfloat16)
    mixed_heads = jnp.einsum(
        "hqk,khd->qhd", weights, value_heads, preferred_element_type=jnp.float32
    )
    mixed_heads = mixed_heads.astype(jnp.bfloat16).reshape(LAT, local_heads * RHD)
    partial_value = jnp.dot(mixed_heads, w_out, preferred_element_type=jnp.float32)
    summed = lax.psum(partial_value, "mp")
    resampled = (latent_init.astype(jnp.float32) + summed).astype(jnp.bfloat16)
    cross_keys = jnp.dot(resampled, wx_key, preferred_element_type=jnp.float32).astype(jnp.bfloat16)
    cross_values = jnp.dot(resampled, wx_value, preferred_element_type=jnp.float32).astype(
        jnp.bfloat16
    )
    cross_width = cross_keys.shape[1]
    cross_heads = cross_width // HD
    key_blocks = cross_keys.reshape(LAT, cross_heads, HD)
    value_blocks = cross_values.reshape(LAT, cross_heads, HD)
    question_count = cites.shape[0]
    cite_count = cites.shape[1]
    requests = question_count * cite_count
    cite_flat = cites.reshape(requests)
    cite_hot = (cite_flat[:, None] == jnp.arange(clip_total, dtype=jnp.int32)[None, :]).astype(
        jnp.int32
    )
    owner_req = jnp.sum(cite_hot * owner_of[None, :], axis=1)
    question_len = queries.shape[0] // question_count
    question_rows = queries.reshape(question_count, question_len, cross_width)
    inv_cross = 1.0 / math.sqrt(HD)
    req_hot = (owner_req[:, None] == jnp.arange(groups, dtype=jnp.int32)[None, :]).astype(jnp.int32)
    req_before = jnp.cumsum(req_hot, axis=0) - req_hot
    req_depth = max(2, 2 * requests // groups)
    req_slot = owner_req * req_depth + jnp.sum(req_before * req_hot, axis=1)
    asker = jnp.arange(requests, dtype=jnp.int32) // cite_count
    send_queries = jnp.zeros((groups * req_depth, question_len, cross_width), jnp.bfloat16)
    send_queries = send_queries.at[req_slot].set(question_rows[asker])
    send_queries = send_queries.reshape(groups, req_depth, question_len, cross_width)
    arrivals = lax.all_to_all(send_queries, "seq", split_axis=0, concat_axis=0, tiled=True)
    block_shape = arrivals.shape
    flat_rows = block_shape[0] * block_shape[1] * block_shape[2]
    query_flat = arrivals.reshape(flat_rows, cross_heads, HD)
    part_scores = (
        jnp.einsum("rhd,khd->rhk", query_flat, key_blocks, preferred_element_type=jnp.float32)
        * inv_cross
    )
    part_max = jnp.max(part_scores, axis=-1)
    part_raised = jnp.exp(part_scores - part_max[..., None])
    part_sum = jnp.sum(part_raised, axis=-1)
    part_out = jnp.einsum(
        "rhk,khd->rhd",
        part_raised.astype(jnp.bfloat16),
        value_blocks,
        preferred_element_type=jnp.float32,
    )
    part_out = part_out.astype(jnp.bfloat16).reshape(block_shape)
    stat_shape = (block_shape[0], block_shape[1], block_shape[2], cross_heads)
    returned_out = lax.all_to_all(part_out, "seq", split_axis=0, concat_axis=0, tiled=True)
    returned_max = lax.all_to_all(
        part_max.reshape(stat_shape), "seq", split_axis=0, concat_axis=0, tiled=True
    )
    returned_sum = lax.all_to_all(
        part_sum.reshape(stat_shape), "seq", split_axis=0, concat_axis=0, tiled=True
    )
    got_out = returned_out
    got_max = returned_max
    got_sum = returned_sum
    got_out = got_out.reshape(groups * req_depth, question_len, cross_width)[req_slot]
    got_max = got_max.reshape(groups * req_depth, question_len, cross_heads)[req_slot]
    got_sum = got_sum.reshape(groups * req_depth, question_len, cross_heads)[req_slot]
    got_out = got_out.reshape(question_count, cite_count, question_len, cross_heads, HD)
    got_max = got_max.reshape(question_count, cite_count, question_len, cross_heads)
    got_sum = got_sum.reshape(question_count, cite_count, question_len, cross_heads)
    merged = merge_parts(got_out, got_max, got_sum)
    context = merged.astype(jnp.bfloat16).reshape(question_count * question_len, cross_width)
    return (resampled, context)


def solution(mesh):
    in_specs = (
        P("seq", None),
        P("seq", None),
        P(),
        P("seq", None),
        P(),
        P(None, "mp"),
        P(None, "mp"),
        P(None, "mp"),
        P("mp", None),
        P(None, "mp"),
        P(None, "mp"),
        P("seq", "mp"),
    )
    out_specs = (P("seq", None), P("seq", "mp"))
    return jax.shard_map(body, mesh=mesh, in_specs=in_specs, out_specs=out_specs, check_vma=False)
```

profile of v0, /device:TPU:1, one launch (start us, length us, event | category | flops | bytes accessed | tf_op | source)
XLA Modules:
  0.0 621.9 jit_solution(16263741768117688256)
XLA Ops:
  11.0 7.6 %scatter_custom_fusion.1 = bf16[2048]{0:T(1024)(128)(2,1)S(1)} fusion(s32[1024]{0:T(1024)S(1)} %bitcast.132, bf16[1024]{0:T(1024)(128)(2,1)S(1)} %broadcast.176, bf16[]{:T(256)} %constant.18.clone.1), kind=kCustom, calls=%fused_computation.76 | custom fusion | bytes 4098 | tf_op jit(solution)/shard_map/scatter | solution.py:55
  20.4 6.3 %all-to-all-start.1 = ((bf16[8,2,128]{2,1,0:T(2,128)(2,1)}), bf16[8,2,128]{2,1,0:T(2,128)(2,1)S(1)}, u32[]{:S(2)}, u32[]{:S(2)}) async-start(bf16[8,2,128]{2,1,0:T(2,128)(2,1)} %reshape.286), calls=%async_computation.1 | async-start | bytes 8192 | tf_op jit(solution)/shard_map/all_to_all | solution.py:60
  26.7 9.3 %scatter_custom_fusion = bf16[2048,1280]{1,0:T(8,128)(2,1)} fusion(s32[1024]{0:T(1024)S(1)} %bitcast.133, bf16[1024,1280]{1,0:T(8,128)(2,1)} %param.12, bf16[]{:T(256)} %constant.18.clone.1), kind=kCustom, calls=%fused_computation.25 | custom fusion | bytes 5243392 | tf_op jit(solution)/shard_map/scatter | solution.py:49
  36.1 5.6 all-to-all-start
  42.3 4.1 gather_fusion
  46.6 4.3 broadcast_in_dim.22
  50.9 19.3 %scatter_fusion = bf16[256,16,1024]{2,1,0:T(8,128)(2,1)} fusion(bf16[256,16,1024]{2,1,0:T(8,128)(2,1)} %broadcast_in_dim.22, s32[128]{0:T(128)S(1)} %fusion.36, bf16[128,16,1024]{2,1,0:T(8,128)(2,1)} %gather_fusion), kind=kCustom, calls=%fused_computation.6 | custom fusion | bytes 12583424 | tf_op jit(solution)/shard_map/scatter | solution.py:126
  70.2 85.8 %all-to-all-done = bf16[8,256,1280]{2,1,0:T(8,128)(2,1)} async-done(((bf16[8,256,1280]{2,1,0:T(8,128)(2,1)}), bf16[8,256,1280]{2,1,0:T(8,128)(2,1)}, u32[]{:S(2)}, u32[]{:S(2)}) %all-to-all-start) | async-done | bytes 5242912 | tf_op jit(solution)/shard_map/all_to_all | solution.py:59
  156.0 5.3 all-to-all-start.2
  166.6 4.6 convolution_convert_fusion
  172.5 3.5 fusion.41
  176.0 4.7 convolution_convert_fusion.1
  183.8 33.8 %all-reduce.3.cloned.1.call-done = f32[64,1280]{1,0:T(8,128)} async-done(((f32[64,1280]{1,0:T(8,128)}), f32[64,1280]{1,0:T(8,128)}) %all-reduce.3.cloned.1.call-update) | async-done | bytes 327696 | tf_op jit(solution)/shard_map/psum | solution.py:99
  219.2 123.5 %all-to-all-done.2 = bf16[8,32,16,1024]{3,2,1,0:T(8,128)(2,1)} async-done(((bf16[8,32,16,1024]{3,2,1,0:T(8,128)(2,1)}), bf16[8,32,16,1024]{3,2,1,0:T(8,128)(2,1)}, u32[]{:S(2)}, u32[]{:S(2)}) %all-to-all-start.2) | async-done | bytes 8388640 | tf_op jit(solution)/shard_map/all_to_all | solution.py:128
  342.7 8.8 %copy.78 = bf16[512,8,8,128]{3,2,1,0:T(8,128)(2,1)} copy(bf16[512,8,8,128]{3,1,2,0:T(8,128)(2,1)} %bitcast.30) | data formatting | bytes 16777216
  351.5 6.4 %bitcast_reduce_fusion = (f32[4096,8]{0,1:T(8,128)S(1)}, f32[8,64,4096]{2,1,0:T(8,128)S(1)}) fusion(bf16[4096,8,128]{2,1,0:T(8,128)(2,1)} %bitcast.113, bf16[8,8,8,128]{3,2,1,0:T(8,128)(2,1)S(1)} %fusion.14), kind=kOutput, calls=%fused_computation.9 | convolution fusion | flops 541032448 | bytes 17039360 | tf_op jit(solution)/shard_map/rhd,khd->rhk/dot_general | solution.py:133
  364.6 5.8 all-to-all-start.5
  379.9 9.0 %convert_bitcast_fusion = bf16[4096,8,128]{0,2,1:T(8,128)(2,1)} fusion(f32[8,64,4096]{2,1,0:T(8,128)} %copy-done.2, f32[4096,8]{0,1:T(8,128)S(1)} %get-tuple-element.6, bf16[8,8,8,128]{3,2,1,0:T(8,128)(2,1)S(1)} %fusion.15), kind=kOutput, calls=%fused_computation.14 | convolution fusion | flops 547356672 | bytes 17039360 | tf_op jit(solution)/shard_map/rhk,khd->rhd/dot_general | solution.py:139
  388.9 12.0 %copy.71 = bf16[4096,8,128]{2,1,0:T(8,128)(2,1)} copy(bf16[4096,8,128]{0,2,1:T(8,128)(2,1)} %convert_bitcast_fusion) | data formatting | bytes 16777216 | tf_op jit(solution)/shard_map/convert_element_type | solution.py:145
  401.0 13.3 %reshape.218 = bf16[8,32,16,1024]{3,2,1,0:T(8,128)(2,1)} reshape(bf16[4096,8,128]{2,1,0:T(8,128)(2,1)} %copy.71) | data formatting | bytes 16777216 | tf_op jit(solution)/shard_map/reshape | solution.py:145
  414.3 5.4 all-to-all-start.4
  428.5 172.0 %all-to-all-done.4 = bf16[8,32,16,1024]{3,2,1,0:T(8,128)(2,1)} async-done(((bf16[8,32,16,1024]{3,2,1,0:T(8,128)(2,1)}), bf16[8,32,16,1024]{3,2,1,0:T(8,128)(2,1)}, u32[]{:S(2)}, u32[]{:S(2)}) %all-to-all-start.4) | async-done | bytes 8388640 | tf_op jit(solution)/shard_map/all_to_all | solution.py:147
  600.5 6.1 gather_fusion.2
  606.6 3.8 copy.79
  (90 shorter events, 47.1 us)
Async XLA Ops:
  7.2 211.5 %copy-start = (bf16[1280,1024]{1,0:T(8,128)(2,1)S(1)}, bf16[1280,1024]{1,0:T(8,128)(2,1)}, u32[]{:S(2)}) copy-start(bf16[1280,1024]{1,0:T(8,128)(2,1)} %param.21) | copy-start | bytes 7864324
  20.4 15.7 %all-to-all-start.1 = ((bf16[8,2,128]{2,1,0:T(2,128)(2,1)}), bf16[8,2,128]{2,1,0:T(2,128)(2,1)S(1)}, u32[]{:S(2)}, u32[]{:S(2)}) async-start(bf16[8,2,128]{2,1,0:T(2,128)(2,1)} %reshape.286), calls=%async_computation.1 | async-start | bytes 8192 | tf_op jit(solution)/shard_map/all_to_all | solution.py:60
  36.1 5.6 copy-start.6
  36.1 5.8 copy-start.7
  36.1 120.0 %all-to-all-start = ((bf16[8,256,1280]{2,1,0:T(8,128)(2,1)}), bf16[8,256,1280]{2,1,0:T(8,128)(2,1)}, u32[]{:S(2)}, u32[]{:S(2)}) async-start(bf16[8,256,1280]{2,1,0:T(8,128)(2,1)} %bitcast.115), calls=%async_computation | async-start | bytes 10485760 | tf_op jit(solution)/shard_map/all_to_all | solution.py:59
  156.0 5.6 copy-start.4
  156.0 186.7 %all-to-all-start.2 = ((bf16[8,32,16,1024]{3,2,1,0:T(8,128)(2,1)}), bf16[8,32,16,1024]{3,2,1,0:T(8,128)(2,1)}, u32[]{:S(2)}, u32[]{:S(2)}) async-start(bf16[8,32,16,1024]{3,2,1,0:T(8,128)(2,1)} %bitcast.112), calls=%async_computation.2 | async-start | bytes 16777216 | tf_op jit(solution)/shard_map/all_to_all | solution.py:128
  161.3 56.3 %all-reduce.3.cloned.1.call-start = ((), (), s32[]{:S(2)}) async-start(), calls=%async_computation.6 | async-start | bytes 655360 | tf_op jit(solution)/shard_map/psum | solution.py:99
  176.0 4.9 copy-start.8
  218.6 151.7 %copy-start.5 = (bf16[64,1280]{1,0:T(8,128)(2,1)}, bf16[64,1280]{1,0:T(8,128)(2,1)S(1)}, u32[]{:S(2)}) copy-start(bf16[64,1280]{1,0:T(8,128)(2,1)S(1)} %add_convert_fusion) | copy-start | bytes 491524
  357.9 3.2 copy-start.2
  364.6 12.0 %all-to-all-start.5 = ((f32[8,1,4096]{2,1,0:T(1,128)}), f32[8,1,4096]{2,1,0:T(1,128)S(1)}, u32[]{:S(2)}, u32[]{:S(2)}) async-start(f32[8,1,4096]{2,1,0:T(1,128)} %reshape.290), calls=%async_computation.5 | async-start | bytes 262144 | tf_op jit(solution)/shard_map/all_to_all | solution.py:151
  376.6 37.7 %all-to-all-start.3 = ((f32[8,1,4096]{2,1,0:T(1,128)}), f32[8,1,4096]{2,1,0:T(1,128)S(1)}, u32[]{:S(2)}, u32[]{:S(2)}) async-start(f32[8,1,4096]{2,1,0:T(1,128)} %reshape.288), calls=%async_computation.3 | async-start | bytes 262144 | tf_op jit(solution)/shard_map/all_to_all | solution.py:148
  414.3 186.2 %all-to-all-start.4 = ((bf16[8,32,16,1024]{3,2,1,0:T(8,128)(2,1)}), bf16[8,32,16,1024]{3,2,1,0:T(8,128)(2,1)}, u32[]{:S(2)}, u32[]{:S(2)}) async-start(bf16[8,32,16,1024]{3,2,1,0:T(8,128)(2,1)} %reshape.218), calls=%async_computation.4 | async-start | bytes 16777216 | tf_op jit(solution)/shard_map/all_to_all | solution.py:147
  606.6 3.8 copy-start.3
  610.4 4.6 copy-start.1
Sparse Core Ops, SparseCore 0:
  183.9 33.6 all-reduce.2
where the time goes:
time: 627 us; the launch traced here: 622 us
  waiting for transfers between devices  417 us (67%)
  local copies, waits for them, and re-layouts  105 us (17%)
  matrix products  38.4 us (6%)
  starting transfers between devices  32 us (5%)
  between operations  14.4 us (2%)
  other arithmetic  14.3 us (2%)
    all_to_all x1, waiting for transfers between devices, body(): lax.all_to_all(part_out, 'seq', split_axis=0, concat_axis=0, tiled=True)  172 us
    all_to_all x1, waiting for transfers between devices, body(): lax.all_to_all(send_queries, 'seq', split_axis=0, concat_axis=0, tiled=True)  123 us
    all_to_all x1, waiting for transfers between devices, body(): lax.all_to_all(outgoing, 'seq', split_axis=0, concat_axis=0, tiled=True)  85.8 us
    psum x1, waiting for transfers between devices, body(): summed = lax.psum(partial_value, 'mp')  33.8 us
    unnamed x28, local copies, waits for them, and re-layouts  19.9 us
    scatter x1, local copies, waits for them, and re-layouts, body(): send_queries = send_queries.at[req_slot].set(question_rows[asker])  19.3 us
    reshape x1, local copies, waits for them, and re-layouts, body(): part_out = part_out.astype(jnp.bfloat16).reshape(block_shape)  13.3 us
  transfers between devices with their start and end apart: 7, of which 5 were waited for; matrix products, arithmetic and copies ran while one was open for 17% of the time, Pallas kernels for 0%

commit v1 on v0

v1 whole, which is shorter than its diff:
```python
import math

import jax
import jax.numpy as jnp
from jax import lax
from jax.sharding import PartitionSpec as P

RHD = 80
LAT = 64
HD = 128

masked_score = -1e30


def split3(x):
    a = x.astype(jnp.bfloat16)
    r = x - a.astype(jnp.float32)
    b = r.astype(jnp.bfloat16)
    c = (r - b.astype(jnp.float32)).astype(jnp.bfloat16)
    return a, b, c


def gather_axis(x, name):
    count = lax.axis_size(name)
    if count & (count - 1):
        return lax.all_gather(x, name, axis=0)
    me = lax.axis_index(name)
    x = x[None]
    step = count // 2
    while step >= 1:
        other = lax.ppermute(x, name, [(i, i ^ step) for i in range(count)])
        low = (me & step) == 0
        x = jnp.where(low, jnp.stack([x, other]), jnp.stack([other, x]))
        x = x.reshape((-1,) + x.shape[2:])
        step //= 2
    bits = count.bit_length() - 1
    order = [int(format(i, "0%db" % bits)[::-1], 2) if bits else 0 for i in range(count)]
    return jnp.stack([x[order[i]] for i in range(count)])


def body(
    patches,
    clip_of,
    owner_of,
    cites,
    latent_init,
    w_query,
    w_key,
    w_value,
    w_out,
    wx_key,
    wx_value,
    queries,
):
    groups = lax.axis_size("seq")
    clip_total = owner_of.shape[0]
    rows = patches.shape[0]
    f32, bf16 = jnp.float32, jnp.bfloat16

    w_out_all = gather_axis(w_out, "mp").reshape(-1, w_out.shape[1])

    clip_hot = (clip_of == jnp.arange(clip_total, dtype=jnp.int32)[None, :]).astype(jnp.int32)
    target = jnp.sum(clip_hot * owner_of[None, :], axis=1)
    key_rows = jnp.dot(patches, w_key, preferred_element_type=f32).astype(bf16)
    value_rows = jnp.dot(patches, w_value, preferred_element_type=f32).astype(bf16)
    lat_q = jnp.dot(latent_init, w_query, preferred_element_type=f32).astype(bf16)
    lat_k = jnp.dot(latent_init, w_key, preferred_element_type=f32).astype(bf16)
    lat_v = jnp.dot(latent_init, w_value, preferred_element_type=f32).astype(bf16)
    heads = lat_q.shape[1] // RHD
    q = lat_q.reshape(LAT, heads, RHD)

    scale = 1.0 / math.sqrt(RHD)
    scores = (
        jnp.einsum("qhd,khd->hqk", q, key_rows.reshape(rows, heads, RHD), preferred_element_type=f32)
        * scale
    )
    member = target[None, :] == jnp.arange(groups, dtype=jnp.int32)[:, None]
    peak = jnp.max(
        jnp.where(member[:, None, None, :], scores[None], masked_score), axis=-1
    )
    raised = jnp.where(
        member[:, None, None, :], jnp.exp(scores[None] - peak[..., None]), 0.0
    )
    total = jnp.sum(raised, axis=-1)
    out = jnp.einsum(
        "ghqk,khd->gqhd",
        raised.astype(bf16),
        value_rows.reshape(rows, heads, RHD),
        preferred_element_type=f32,
    )
    safe = jnp.where(total > 0, total, 1.0)
    out = out / jnp.swapaxes(safe, 1, 2)[..., None]
    lse = jnp.where(total > 0, peak + jnp.log(safe), masked_score)
    lse = jnp.swapaxes(lse, 1, 2)
    pad = 384 - heads * RHD - 3 * heads
    packed = jnp.concatenate(
        [out.reshape(groups, LAT, heads * RHD).astype(bf16)]
        + list(split3(lse))
        + [jnp.zeros((groups, LAT, pad), bf16)],
        axis=-1,
    )
    got = lax.all_to_all(packed, "seq", split_axis=0, concat_axis=0, tiled=True)
    width = heads * RHD
    got_out = got[..., :width].astype(f32).reshape(groups, LAT, heads, RHD)
    tail = got[..., width : width + 3 * heads].astype(f32).reshape(groups, LAT, 3, heads)
    got_lse = tail[:, :, 0] + tail[:, :, 1] + tail[:, :, 2]

    lat_scores = (
        jnp.einsum("qhd,khd->qhk", q, lat_k.reshape(LAT, heads, RHD), preferred_element_type=f32)
        * scale
    )
    lat_peak = jnp.max(lat_scores, axis=-1)
    lat_raised = jnp.exp(lat_scores - lat_peak[..., None])
    lat_total = jnp.sum(lat_raised, axis=-1)
    lat_out = jnp.einsum(
        "qhk,khd->qhd",
        lat_raised.astype(bf16),
        lat_v.reshape(LAT, heads, RHD),
        preferred_element_type=f32,
    )
    best = jnp.maximum(jnp.max(got_lse, axis=0), lat_peak)
    lat_w = jnp.exp(lat_peak - best)
    part_w = jnp.exp(got_lse - best[None])
    denominator = lat_w * lat_total + jnp.sum(part_w, axis=0)
    numerator = lat_w[..., None] * lat_out + jnp.sum(part_w[..., None] * got_out, axis=0)
    mixed = (numerator / denominator[..., None]).astype(bf16).reshape(LAT, width)

    mixed_all = gather_axis(gather_axis(mixed, "seq"), "mp")
    mixed_all = jnp.moveaxis(mixed_all, 0, 2).reshape(groups * LAT, -1)
    latents = jnp.dot(mixed_all, w_out_all, preferred_element_type=f32)
    latents = latents.reshape(groups, LAT, -1) + latent_init.astype(f32)[None]
    latents = latents.astype(bf16)
    resampled = lax.dynamic_index_in_dim(latents, lax.axis_index("seq"), 0, keepdims=False)
    latents = latents.reshape(groups * LAT, -1)

    cross_keys = jnp.dot(latents, wx_key, preferred_element_type=f32).astype(bf16)
    cross_values = jnp.dot(latents, wx_value, preferred_element_type=f32).astype(bf16)
    cross_heads = cross_keys.shape[1] // HD
    question_count = cites.shape[0]
    question_len = queries.shape[0] // question_count
    cite_hot = cites[:, :, None] == jnp.arange(clip_total, dtype=jnp.int32)[None, None, :]
    cite_owner = jnp.sum(cite_hot * owner_of[None, None, :], axis=2)
    cited = jnp.any(
        cite_owner[:, :, None] == jnp.arange(groups, dtype=jnp.int32)[None, None, :], axis=1
    )
    token_cited = jnp.repeat(cited, question_len, axis=0)
    key_cited = jnp.repeat(token_cited, LAT, axis=1)
    q_heads = queries.reshape(-1, cross_heads, HD)
    s = jnp.einsum(
        "thd,khd->htk", q_heads, cross_keys.reshape(-1, cross_heads, HD), preferred_element_type=f32
    ) * (1.0 / math.sqrt(HD))
    s = jnp.where(key_cited[None], s, masked_score)
    top = jnp.max(s, axis=-1, keepdims=True)
    p = jnp.exp(s - top)
    denom = jnp.sum(p, axis=-1)
    ctx = jnp.einsum(
        "htk,khd->thd",
        p.astype(bf16),
        cross_values.reshape(-1, cross_heads, HD),
        preferred_element_type=f32,
    )
    ctx = ctx / denom.T[..., None]
    return (resampled, ctx.astype(bf16).reshape(queries.shape))


def solution(mesh):
    in_specs = (
        P("seq", None),
        P("seq", None),
        P(),
        P("seq", None),
        P(),
        P(None, "mp"),
        P(None, "mp"),
        P(None, "mp"),
        P("mp", None),
        P(None, "mp"),
        P(None, "mp"),
        P("seq", "mp"),
    )
    out_specs = (P("seq", None), P("seq", "mp"))
    return jax.shard_map(body, mesh=mesh, in_specs=in_specs, out_specs=out_specs, check_vma=False)
```

time: 627 us -> 118 us (0.19)
  waiting for transfers between devices: 417 us -> 11.3 us
  local copies, waits for them, and re-layouts: 105 us -> 34.6 us
  between operations: 14.4 us -> 0.97 us
  matrix products: 38.4 us -> 26.3 us
  starting transfers between devices: 32 us -> 21 us
  other arithmetic: 14.3 us -> 22.5 us
    all_to_all x6 -> x1, waiting for transfers between devices: 384 us -> 1.59 us  [body(): got = lax.all_to_all(packed, 'seq', split_axis=0, concat_axis=0, tiled=True)]
    scatter x3 -> x0, local copies, waits for them, and re-layouts: 36.2 us -> none  [the longest x1 19.3 us: body(): send_queries = send_queries.at[req_slot].set(question_rows[asker])]
    psum x1 -> x0, waiting for transfers between devices: 33.8 us -> none  [body(): summed = lax.psum(partial_value, 'mp')]
    all_to_all x6 -> x1, starting transfers between devices: 31.7 us -> 6.34 us  [body(): got = lax.all_to_all(packed, 'seq', split_axis=0, concat_axis=0, tiled=True)]
    ppermute x0 -> x7, starting transfers between devices: none -> 14.7 us  [gather_axis(): other = lax.ppermute(x, name, [(i, i ^ step) for i in range(count)])]
    gather x4 -> x0, local copies, waits for them, and re-layouts: 12.8 us -> none  [the longest x1 6.12 us: body(): got_out.reshape(groups * req_depth, question_len, cross_width)[req_slot]]
    reshape x7 -> x5, local copies, waits for them, and re-layouts: 15.2 us -> 3.96 us  [the longest x1 2.29 us: body(): cross_values.reshape(-1, cross_heads, HD)]
    select_n x3 -> x10, other arithmetic: 0.02 us -> 11.2 us  [gather_axis(): x = jnp.where(low, jnp.stack([x, other]), jnp.stack([other, x]))]
  transfers between devices with their start and end apart: 7 -> 8, of which waited for: 5 -> 4; matrix products, arithmetic and copies ran while one was open for 17% -> 33% of each run, Pallas kernels for 0% -> 0%
where the time goes in v1:
time: 118 us; the launch traced here: 117 us
  local copies, waits for them, and re-layouts  34.6 us (29%)
  matrix products  26.3 us (22%)
  other arithmetic  22.5 us (19%)
  starting transfers between devices  21 us (18%)
  waiting for transfers between devices  11.3 us (10%)
    ppermute x7, starting transfers between devices, gather_axis(): other = lax.ppermute(x, name, [(i, i ^ step) for i in range(count)])  14.7 us
    select_n x10, other arithmetic, gather_axis(): x = jnp.where(low, jnp.stack([x, other]), jnp.stack([other, x]))  11.2 us
    unnamed x36, local copies, waits for them, and re-layouts  10.1 us
    ppermute x7, waiting for transfers between devices, gather_axis(): other = lax.ppermute(x, name, [(i, i ^ step) for i in range(count)])  9.69 us
    all_to_all x1, starting transfers between devices, body(): got = lax.all_to_all(packed, 'seq', split_axis=0, concat_axis=0, tiled=True)  6.34 us
    mul x2, local copies, waits for them, and re-layouts, body(): part_w[..., None] * got_out  5.12 us
    dot_general x1, matrix products, body(): jnp.einsum('htk,khd->thd', p.astype(bf16), cross_values.reshape(-1, cross...  3.57 us
    convert_element_type x2, local copies, waits for them, and re-layouts, body(): out.reshape(groups, LAT, heads * RHD).astype(bf16)  3.39 us
  transfers between devices with their start and end apart: 8, of which 4 were waited for; matrix products, arithmetic and copies ran while one was open for 33% of the time, Pallas kernels for 0%

profile of v1, /device:TPU:1, one launch (start us, length us, event | category | flops | bytes accessed | tf_op | source)
XLA Modules:
  0.0 116.7 jit_solution(10236550144200708063)
XLA Ops:
  3.3 2.2 %convolution_convert_fusion.2 = bf16[1024,320]{0,1:T(8,128)(2,1)S(1)} fusion(bf16[1024,1280]{1,0:T(8,128)(2,1)S(1)} %copy-done, bf16[1280,320]{0,1:T(8,128)(2,1)} %param.18), kind=kOutput, calls=%fused_computation.48 | convolution fusion | flops 839188480 | bytes 4096000 | tf_op jit(solution)/shard_map/dot_general | solution.py:64
  6.8 2.1 %fusion = f32[8,4,64]{2,0,1:T(8,128)S(1)} fusion(f32[8,4,64]{2,0,1:T(8,128)S(1)} %select_reduce_fusion, f32[4,64,1024]{2,1,0:T(8,128)S(1)} %convolution_multiply_fusion, pred[8,1024]{1,0:T(8,128)(4,1)S(1)} %iota_compare_fusion), kind=kLoop, calls=%fused_computation.3 | loop fusion | flops 6289408 | bytes 1073152 | tf_op jit(solution)/shard_map/reduce_sum | solution.py:84
  16.1 2.2 %convert_element_type.75 = bf16[8,64,320]{2,1,0:T(8,128)(2,1)} reshape(bf16[8,64,4,80]{3,2,1,0:T(4,128)(2,1)} %copy.115) | data formatting | bytes 655360 | tf_op jit(solution)/shard_map/convert_element_type | solution.py:97
  18.9 2.1 %concatenate.63 = bf16[8,64,384]{2,1,0:T(8,128)(2,1)} concatenate(bf16[8,64,320]{2,1,0:T(8,128)(2,1)} %convert_element_type.75, bf16[8,64,4]{2,1,0:T(8,128)(2,1)} %copy.116, bf16[8,64,4]{2,1,0:T(8,128)(2,1)} %copy.117, bf16[8,64,4]{2,1,0:T(8,128)(2,1)} %copy.118, bf16[8,64,52]{2,1,0:T(8,128)(2,1)} %broadcast_in_dim.92), dimensions={2} | concatenate | bytes 786432 | tf_op jit(solution)/shard_map/concatenate | solution.py:96
  21.0 6.3 %all-to-all-start = ((bf16[8,64,384]{2,1,0:T(8,128)(2,1)}), bf16[8,64,384]{2,1,0:T(8,128)(2,1)}, u32[]{:S(2)}, u32[]{:S(2)}) async-start(bf16[8,64,384]{2,1,0:T(8,128)(2,1)} %concatenate.63), calls=%async_computation | async-start | bytes 786432 | tf_op jit(solution)/shard_map/all_to_all | solution.py:102
  40.2 2.5 %mul.75 = f32[8,64,4,80]{3,2,1,0:T(4,128)} broadcast(f32[8,64,4]{2,1,0:T(8,128)} %copy.122), dimensions={0,1,2} | broadcast | bytes 663552 | tf_op jit(solution)/shard_map/mul | solution.py:125
  42.7 2.6 %mul.76 = f32[8,64,320]{2,1,0:T(8,128)} reshape(f32[8,64,4,80]{3,2,1,0:T(4,128)} %mul.75) | data formatting | bytes 1310720 | tf_op jit(solution)/shard_map/mul | solution.py:125
  50.5 2.9 %collective-permute-start = (bf16[1,64,320]{2,1,0:T(8,128)(2,1)S(1)}, bf16[1,64,320]{2,1,0:T(8,128)(2,1)}, u32[]{:S(2)}, u32[]{:S(2)}) collective-permute-start(bf16[1,64,320]{2,1,0:T(8,128)(2,1)S(1)} %broadcast_in_dim_reshape.4), channel_id=1, source_target_pairs={{0,16},{4,20},{8,24},{12,28},{16,0},{20,4},{24,8},{28,12},{1,17},{... | collective-permute-start | bytes 122888 | tf_op jit(solution)/shard_map/ppermute | solution.py:31
  57.5 2.5 %collective-permute-done.1 = bf16[2,64,320]{2,1,0:T(8,128)(2,1)S(1)} collective-permute-done((bf16[2,64,320]{2,1,0:T(8,128)(2,1)S(1)}, bf16[2,64,320]{2,1,0:T(8,128)(2,1)S(1)}, u32[]{:S(2)}, u32[]{:S(2)}) %collective-permute-start.1) | collective-permute-done | bytes 81952 | tf_op jit(solution)/shard_map/ppermute | solution.py:31
  60.1 2.3 %collective-permute-start.2 = (bf16[4,64,320]{2,1,0:T(8,128)(2,1)S(1)}, bf16[4,64,320]{2,1,0:T(8,128)(2,1)S(1)}, u32[]{:S(2)}, u32[]{:S(2)}) collective-permute-start(bf16[4,64,320]{2,1,0:T(8,128)(2,1)S(1)} %bitcast.162), channel_id=1, source_target_pairs={{0,4},{4,0},{8,12},{12,8},{16,20},{20,16},{24,28},{28,24},{1,5},{5... | collective-permute-start | bytes 491528 | tf_op jit(solution)/shard_map/ppermute | solution.py:31
  62.4 2.8 %maximum_select_fusion.2 = bf16[2,320,1280]{2,1,0:T(8,128)(2,1)} fusion(bf16[1,320,1280]{2,1,0:T(8,128)(2,1)} %collective-permute-done.5, bf16[1,320,1280]{2,1,0:T(8,128)(2,1)S(1)} %bitcast.147, pred[]{:T(512)S(6)} %eq.76), kind=kLoop, calls=%fused_computation.34 | loop fusion | flops 2457600 | bytes 3276801 | tf_op jit(solution)/shard_map/jit(_where)/select_n | solution.py:33
  65.2 4.0 %collective-permute-start.6 = (bf16[2,320,1280]{2,1,0:T(8,128)(2,1)}, bf16[2,320,1280]{2,1,0:T(8,128)(2,1)}, u32[]{:S(2)}, u32[]{:S(2)}) collective-permute-start(bf16[2,320,1280]{2,1,0:T(8,128)(2,1)} %maximum_select_fusion.2), channel_id=1, source_target_pairs={{0,1},{1,0},{2,3},{3,2},{4,5},{5,4},{6,7},{7,6},{8,9},{9,8},{10,11... | collective-permute-start | bytes 4915208 | tf_op jit(solution)/shard_map/ppermute | solution.py:31
  77.6 5.8 %collective-permute-done.3 = bf16[1,8,64,320]{3,2,0,1:T(8,128)(2,1)} collective-permute-done((bf16[1,8,64,320]{3,2,0,1:T(8,128)(2,1)}, bf16[1,8,64,320]{3,2,0,1:T(8,128)(2,1)}, u32[]{:S(2)}, u32[]{:S(2)}) %collective-permute-start.3) | collective-permute-done | bytes 327712 | tf_op jit(solution)/shard_map/ppermute | solution.py:31
  85.1 2.8 %collective-permute-start.4 = (bf16[2,8,64,320]{3,2,0,1:T(8,128)(2,1)S(1)}, bf16[2,8,64,320]{3,2,0,1:T(8,128)(2,1)S(1)}, u32[]{:S(2)}, u32[]{:S(2)}) collective-permute-start(bf16[2,8,64,320]{3,2,0,1:T(8,128)(2,1)S(1)} %maximum_select_fusion.4), channel_id=1, source_target_pairs={{0,1},{1,0},{2,3},{3,2},{4,5},{5,4},{6,7},{7,6},{8,9},{9,8},{10,11... | collective-permute-start | bytes 1966088 | tf_op jit(solution)/shard_map/ppermute | solution.py:31
  89.6 1.7 %pad_maximum_fusion = (bf16[1,2,8,64,320]{4,3,2,1,0:T(8,128)(2,1)S(1)}, bf16[1,2,8,64,320]{4,3,2,1,0:T(8,128)(2,1)S(1)}) fusion(bf16[1,1,8,64,320]{4,3,2,1,0:T(8,128)(2,1)} %bitcast.22, bf16[1,1,8,64,320]{4,3,2,1,0:T(8,128)(2,1)} %bitcast.20), kind=kLoop, calls=%fused_computation.66 | loop fusion | flops 655360 | bytes 1966080 | tf_op jit(solution)/shard_map/stack | solution.py:33
  92.1 2.4 %maximum_select_fusion = bf16[2,2,320,1280]{3,2,1,0:T(8,128)(2,1)S(1)} fusion(bf16[1,2,320,1280]{3,2,1,0:T(8,128)(2,1)} %bitcast.29, bf16[1,2,320,1280]{3,2,1,0:T(8,128)(2,1)S(1)} %maximum_select_fusion.1, pred[]{:T(512)S(6)} %eq.75), kind=kLoop, calls=%fused_computation.19 | loop fusion | flops 4915200 | bytes 6553601 | tf_op jit(solution)/shard_map/jit(_where)/select_n | solution.py:33
  95.5 2.2 %fusion.26 = bf16[8,64,1280]{2,1,0:T(8,128)(2,1)S(1)} fusion(bf16[1,320,1280]{2,1,0:T(8,128)(2,1)S(1)} %get-tuple-element.19, bf16[1,320,1280]{2,1,0:T(8,128)(2,1)S(1)} %get-tuple-element.20, bf16[1,320,1280]{2,1,0:T(8,128)(2,1)S(1)} %get-tuple-element.21, bf16[1,320,1280]{2,1,0:T(8,128)(2,1)S(1)} %get-tuple-element.18, ...), kind=kOutput, calls=%fused_computation.30 | convolution fusion | flops 1685913600 | bytes 6225920 | tf_op jit(solution)/shard_map/dot_general | solution.py:130
  98.4 2.6 %fusion.36 = bf16[64,8,8,128]{3,2,1,0:T(8,128)(2,1)} fusion(bf16[512,1280]{1,0:T(8,128)(2,1)S(1)} %bitcast.170, bf16[1280,1024]{1,0:T(8,128)(2,1)S(1)} %copy-done.11), kind=kOutput, calls=%fused_computation.45 | convolution fusion | flops 1342701568 | bytes 4980736 | tf_op jit(solution)/shard_map/dot_general | solution.py:136
  101.0 2.5 %convolution_convert_fusion.1 = bf16[512,1024]{1,0:T(8,128)(2,1)} fusion(bf16[512,1280]{1,0:T(8,128)(2,1)S(1)} %bitcast.171, bf16[1280,1024]{1,0:T(8,128)(2,1)S(1)} %copy-done.12), kind=kOutput, calls=%fused_computation.44 | convolution fusion | flops 1342701568 | bytes 4980736 | tf_op jit(solution)/shard_map/dot_general | solution.py:137
  103.5 2.3 %copy.141 = bf16[512,1024]{0,1:T(8,128)(2,1)} copy(bf16[512,1024]{1,0:T(8,128)(2,1)} %convolution_convert_fusion.1) | data formatting | bytes 2097152 | tf_op jit(solution)/shard_map/reshape | solution.py:159
  105.9 3.2 %fusion.4 = (f32[8,512]{1,0:T(8,128)S(1)}, f32[8,512,512]{2,1,0:T(8,128)S(1)}) fusion(pred[512,512]{0,1:T(8,128)(4,1)S(1)} %bitcast.157, bf16[64,8,8,128]{3,2,1,0:T(8,128)(2,1)} %fusion.36, bf16[512,1024]{1,0:T(8,128)(2,1)} %param.23), kind=kOutput, calls=%fused_computation.8 | convolution fusion | flops 543158272 | bytes 10764288 | tf_op jit(solution)/shard_map/thd,khd->htk/dot_general | solution.py:149
  109.1 1.8 %fusion.2 = f32[8,512]{1,0:T(8,128)S(1)} fusion(f32[8,512,512]{2,1,0:T(8,128)S(1)} %get-tuple-element.35, f32[8,512]{1,0:T(8,128)S(1)} %get-tuple-element.34, pred[512,512]{0,1:T(8,128)(4,1)S(1)} %bitcast.158), kind=kLoop, calls=%fused_computation.6 | loop fusion | flops 8384512 | bytes 8683520 | tf_op jit(solution)/shard_map/reduce_sum | solution.py:155
  110.9 3.6 %fusion.27 = bf16[512,8,128]{0,2,1:T(8,128)(2,1)} fusion(bf16[512,8,128]{0,2,1:T(8,128)(2,1)S(1)} %bitcast.160, f32[8,512,512]{2,1,0:T(8,128)S(1)} %get-tuple-element.35, f32[8,512]{1,0:T(8,128)S(1)} %get-tuple-element.34, pred[512,512]{0,1:T(8,128)(4,1)S(1)} %bitcast.159, f32[512,8]{0,1:T(8,128)S(1)} %bitcast.172), kind=kOutput, calls=%fused_computation.32 | convolution fusion | flops 546308096 | bytes 10780672 | tf_op jit(solution)/shard_map/htk,khd->thd/dot_general | solution.py:156
  114.4 2.3 %copy.134 = bf16[512,1024]{1,0:T(8,128)(2,1)} copy(bf16[512,1024]{0,1:T(8,128)(2,1)} %bitcast.161) | data formatting | bytes 2097152
  (95 shorter events, 48.1 us)
Async XLA Ops:
  0.6 2.7 %copy-start = (bf16[1024,1280]{1,0:T(8,128)(2,1)S(1)}, bf16[1024,1280]{1,0:T(8,128)(2,1)}, u32[]{:S(2)}) copy-start(bf16[1024,1280]{1,0:T(8,128)(2,1)} %param.12) | copy-start | bytes 7864324
  5.8 1.0 copy-start.1
  5.8 6.1 %copy-start.5 = (bf16[1280,320]{0,1:T(8,128)(2,1)S(1)}, bf16[1280,320]{0,1:T(8,128)(2,1)}, u32[]{:S(2)}) copy-start(bf16[1280,320]{0,1:T(8,128)(2,1)} %param.19) | copy-start | bytes 2457604
  11.9 1.2 %copy-start.2 = (f32[4,64,1024]{2,1,0:T(8,128)S(1)}, f32[4,64,1024]{2,1,0:T(8,128)}, u32[]{:S(2)}) copy-start(f32[4,64,1024]{2,1,0:T(8,128)} %copy-done.1) | copy-start | bytes 3145732
  11.9 1.2 %copy-start.8 = (f32[8,64,4]{1,0,2:T(8,128)S(1)}, f32[8,64,4]{1,0,2:T(8,128)}, u32[]{:S(2)}) copy-start(f32[8,64,4]{1,0,2:T(8,128)} %get-tuple-element.31) | copy-start | bytes 24580
  14.8 12.5 %copy-start.3 = (bf16[320,1280]{1,0:T(8,128)(2,1)S(1)}, bf16[320,1280]{1,0:T(8,128)(2,1)}, u32[]{:S(2)}) copy-start(bf16[320,1280]{1,0:T(8,128)(2,1)} %param.20) | copy-start | bytes 2457604
  21.0 15.6 %all-to-all-start = ((bf16[8,64,384]{2,1,0:T(8,128)(2,1)}), bf16[8,64,384]{2,1,0:T(8,128)(2,1)}, u32[]{:S(2)}, u32[]{:S(2)}) async-start(bf16[8,64,384]{2,1,0:T(8,128)(2,1)} %concatenate.63), calls=%async_computation | async-start | bytes 786432 | tf_op jit(solution)/shard_map/all_to_all | solution.py:102
  27.3 35.1 %collective-permute-start.5 = (bf16[1,320,1280]{2,1,0:T(8,128)(2,1)S(1)}, bf16[1,320,1280]{2,1,0:T(8,128)(2,1)}, u32[]{:S(2)}, u32[]{:S(2)}) collective-permute-start(bf16[1,320,1280]{2,1,0:T(8,128)(2,1)S(1)} %bitcast.146), channel_id=1, source_target_pairs={{0,2},{1,3},{2,0},{3,1},{4,6},{5,7},{6,4},{7,5},{8,10},{9,11},{10,... | collective-permute-start | bytes 2457608 | tf_op jit(solution)/shard_map/ppermute | solution.py:31
  34.3 0.7 copy-start.6
  50.5 5.0 %collective-permute-start = (bf16[1,64,320]{2,1,0:T(8,128)(2,1)S(1)}, bf16[1,64,320]{2,1,0:T(8,128)(2,1)}, u32[]{:S(2)}, u32[]{:S(2)}) collective-permute-start(bf16[1,64,320]{2,1,0:T(8,128)(2,1)S(1)} %broadcast_in_dim_reshape.4), channel_id=1, source_target_pairs={{0,16},{4,20},{8,24},{12,28},{16,0},{20,4},{24,8},{28,12},{1,17},{... | collective-permute-start | bytes 122888 | tf_op jit(solution)/shard_map/ppermute | solution.py:31
  56.4 3.5 %collective-permute-start.1 = (bf16[2,64,320]{2,1,0:T(8,128)(2,1)S(1)}, bf16[2,64,320]{2,1,0:T(8,128)(2,1)S(1)}, u32[]{:S(2)}, u32[]{:S(2)}) collective-permute-start(bf16[2,64,320]{2,1,0:T(8,128)(2,1)S(1)} %maximum_select_fusion.8), channel_id=1, source_target_pairs={{0,8},{4,12},{8,0},{12,4},{16,24},{20,28},{24,16},{28,20},{1,9},{5... | collective-permute-start | bytes 245768 | tf_op jit(solution)/shard_map/ppermute | solution.py:31
  60.0 17.2 %copy-start.9 = (s32[8]{0:T(128)S(1)}, s32[8]{0:T(128)}, u32[]{:S(2)}) copy-start(s32[8]{0:T(128)} %param.14) | copy-start | bytes 100
  60.1 17.2 %copy-start.10 = (s32[32,4]{0,1:T(4,128)S(1)}, s32[32,4]{0,1:T(4,128)}, u32[]{:S(2)}) copy-start(s32[32,4]{0,1:T(4,128)} %param.15) | copy-start | bytes 1540
  60.1 9.1 %collective-permute-start.2 = (bf16[4,64,320]{2,1,0:T(8,128)(2,1)S(1)}, bf16[4,64,320]{2,1,0:T(8,128)(2,1)S(1)}, u32[]{:S(2)}, u32[]{:S(2)}) collective-permute-start(bf16[4,64,320]{2,1,0:T(8,128)(2,1)S(1)} %bitcast.162), channel_id=1, source_target_pairs={{0,4},{4,0},{8,12},{12,8},{16,20},{20,16},{24,28},{28,24},{1,5},{5... | collective-permute-start | bytes 491528 | tf_op jit(solution)/shard_map/ppermute | solution.py:31
  65.2 26.9 %collective-permute-start.6 = (bf16[2,320,1280]{2,1,0:T(8,128)(2,1)}, bf16[2,320,1280]{2,1,0:T(8,128)(2,1)}, u32[]{:S(2)}, u32[]{:S(2)}) collective-permute-start(bf16[2,320,1280]{2,1,0:T(8,128)(2,1)} %maximum_select_fusion.2), channel_id=1, source_target_pairs={{0,1},{1,0},{2,3},{3,2},{4,5},{5,4},{6,7},{7,6},{8,9},{9,8},{10,11... | collective-permute-start | bytes 4915208 | tf_op jit(solution)/shard_map/ppermute | solution.py:31
  74.3 9.1 %collective-permute-start.3 = (bf16[1,8,64,320]{3,2,0,1:T(8,128)(2,1)}, bf16[1,8,64,320]{3,2,0,1:T(8,128)(2,1)}, u32[]{:S(2)}, u32[]{:S(2)}) collective-permute-start(bf16[1,8,64,320]{3,2,0,1:T(8,128)(2,1)} %bitcast.21), channel_id=1, source_target_pairs={{0,2},{1,3},{2,0},{3,1},{4,6},{5,7},{6,4},{7,5},{8,10},{9,11},{10,... | collective-permute-start | bytes 983048 | tf_op jit(solution)/shard_map/ppermute | solution.py:31
  85.1 6.3 %collective-permute-start.4 = (bf16[2,8,64,320]{3,2,0,1:T(8,128)(2,1)S(1)}, bf16[2,8,64,320]{3,2,0,1:T(8,128)(2,1)S(1)}, u32[]{:S(2)}, u32[]{:S(2)}) collective-permute-start(bf16[2,8,64,320]{3,2,0,1:T(8,128)(2,1)S(1)} %maximum_select_fusion.4), channel_id=1, source_target_pairs={{0,1},{1,0},{2,3},{3,2},{4,5},{5,4},{6,7},{7,6},{8,9},{9,8},{10,11... | collective-permute-start | bytes 1966088 | tf_op jit(solution)/shard_map/ppermute | solution.py:31
  94.6 1.0 copy-start.7
  95.5 2.9 %copy-start.11 = (bf16[1280,1024]{1,0:T(8,128)(2,1)S(1)}, bf16[1280,1024]{1,0:T(8,128)(2,1)}, u32[]{:S(2)}) copy-start(bf16[1280,1024]{1,0:T(8,128)(2,1)} %param.21) | copy-start | bytes 7864324
  98.4 2.6 %copy-start.12 = (bf16[1280,1024]{1,0:T(8,128)(2,1)S(1)}, bf16[1280,1024]{1,0:T(8,128)(2,1)}, u32[]{:S(2)}) copy-start(bf16[1280,1024]{1,0:T(8,128)(2,1)} %param.22) | copy-start | bytes 7864324
  109.1 1.8 %copy-start.4 = (bf16[512,1024]{0,1:T(8,128)(2,1)S(1)}, bf16[512,1024]{0,1:T(8,128)(2,1)}, u32[]{:S(2)}) copy-start(bf16[512,1024]{0,1:T(8,128)(2,1)} %copy.141) | copy-start | bytes 3145732

commit v2 on v1

v2 whole, which is shorter than its diff:
```python
import functools
import math

import jax
import jax.numpy as jnp
from jax import lax
from jax.experimental import pallas as pl
from jax.experimental.pallas import tpu as pltpu
from jax.sharding import PartitionSpec as P

RHD = 80
LAT = 64
HD = 128
KEYS = 512

masked_score = -1e30
f32 = jnp.float32
bf16 = jnp.bfloat16


def matmul(a, b):
    return jnp.dot(a, b, preferred_element_type=f32)


def matmul_nt(a, b):
    return lax.dot_general(a, b, (((1,), (1,)), ((), ())), preferred_element_type=f32)


def split3(x):
    a = x.astype(bf16).astype(f32)
    b = (x - a).astype(bf16).astype(f32)
    return a, b, x - a - b


def finish(out, peak, total, heads):
    safe = jnp.where(total > 0, total, 1.0)
    lse = jnp.where(total > 0, peak + jnp.log(safe), masked_score)
    cols = [out[h] / safe[h * LAT : (h + 1) * LAT] for h in range(heads)]
    for part in split3(lse):
        cols += [part[h * LAT : (h + 1) * LAT] for h in range(heads)]
    cols.append(jnp.zeros((LAT, 384 - heads * (RHD + 3)), f32))
    return jnp.concatenate(cols, axis=1)


def partial_kernel(
    owner_ref, clip_ref, patches_ref, lat_ref, wq_ref, wk_ref, wv_ref,
    out_ref, lat_out_ref, qbd, scores, values, masked, peaks,
):
    step = pl.program_id(0)
    block = patches_ref.shape[0]
    width = wq_ref.shape[1]
    heads = width // RHD
    clips = owner_ref.shape[0]
    scale = 1.0 / math.sqrt(RHD)

    @pl.when(step == 0)
    def _():
        lat = lat_ref[...]
        q = matmul(lat, wq_ref[...])
        lane = lax.broadcasted_iota(jnp.int32, q.shape, 1)
        for h in range(heads):
            inside = (lane >= h * RHD) & (lane < (h + 1) * RHD)
            qbd[h * LAT : (h + 1) * LAT, :] = jnp.where(inside, q, 0.0).astype(bf16)
        lk = matmul(lat, wk_ref[...]).astype(bf16)
        lv = matmul(lat, wv_ref[...]).astype(bf16)
        s = matmul_nt(qbd[...], lk) * scale
        peak = jnp.max(s, axis=1, keepdims=True)
        p = jnp.exp(s - peak)
        total = jnp.sum(p, axis=1, keepdims=True)
        pb = p.astype(bf16)
        out = [
            matmul(pb[h * LAT : (h + 1) * LAT], lv[:, h * RHD : (h + 1) * RHD])
            for h in range(heads)
        ]
        lat_out_ref[...] = finish(out, peak, total, heads)

    x = patches_ref[...]
    kb = matmul(x, wk_ref[...]).astype(bf16)
    vb = matmul(x, wv_ref[...]).astype(bf16)
    here = pl.ds(pl.multiple_of(step * block, block), block)
    scores[:, here] = matmul_nt(qbd[...], kb) * scale
    for h in range(heads):
        values[h, here, :] = vb[:, h * RHD : (h + 1) * RHD]

    @pl.when(step == pl.num_programs(0) - 1)
    def _():
        clip = clip_ref[...]
        few = clips <= 8

        def find_peak(c, selected):
            s = scores[...]
            inside = clip == c
            peak = jnp.max(jnp.where(inside, s, masked_score), axis=1, keepdims=True)
            peaks[c] = peak
            return jnp.where(inside, peak, selected)

        selected = lax.fori_loop(
            0, clips, find_peak, jnp.zeros(scores.shape, f32), unroll=few
        )
        p = jnp.exp(scores[...] - selected)
        scores[...] = p
        pb = p.astype(bf16)
        group = masked.shape[1] // LAT

        def one_group(base, carry):
            totals = []
            for k in range(group):
                c = base * group + k
                inside = clip == c
                totals.append(
                    jnp.sum(jnp.where(inside, scores[...], 0.0), axis=1, keepdims=True)
                )
                keep = jnp.where(inside, 1.0, 0.0).astype(bf16)
                pc = scores[...].astype(bf16) * keep
                for h in range(heads):
                    masked[h, k * LAT : (k + 1) * LAT, :] = pc[h * LAT : (h + 1) * LAT]
            outs = [matmul(masked[h], values[h]) for h in range(heads)]
            for k in range(group):
                c = base * group + k
                out = [o[k * LAT : (k + 1) * LAT] for o in outs]
                out_ref[owner_ref[c]] = finish(out, peaks[c], totals[k], heads).astype(bf16)
            return carry

        lax.fori_loop(0, clips // group, one_group, 0, unroll=few)


def merge_kernel(got_ref, lat_ref, out_ref):
    groups = got_ref.shape[0]
    heads = 4
    width = heads * RHD

    def stats(tail):
        return sum(tail[:, i * heads : (i + 1) * heads] for i in range(3))

    def spread(w):
        lane = lax.broadcasted_iota(jnp.int32, (LAT, width), 1)
        full = jnp.broadcast_to(w[:, 0:1], (LAT, width))
        for h in range(1, heads):
            full = jnp.where(lane >= h * RHD, w[:, h : h + 1], full)
        return full

    lat_lse = stats(lat_ref[:, width : width + 3 * heads])
    lse = [
        stats(got_ref[g, :, width : width + 3 * heads].astype(f32)) for g in range(groups)
    ]
    best = functools.reduce(jnp.maximum, lse, lat_lse)
    weights = [jnp.exp(x - best) for x in lse]
    lat_weight = jnp.exp(lat_lse - best)
    total = sum(weights, lat_weight)
    mixed = spread(lat_weight / total) * lat_ref[:, :width]
    for g in range(groups):
        mixed = mixed + spread(weights[g] / total) * got_ref[g, :, :width].astype(f32)
    half = LAT // 2
    third = jnp.concatenate([mixed[:half, 256:320], mixed[half:, 256:320]], axis=1)
    packed = jnp.concatenate([mixed[:, :128], mixed[:, 128:256], third], axis=0).astype(bf16)
    for g in range(groups):
        out_ref[g] = packed


def cross_kernel(*refs, blocks, ways):
    mix = refs[:ways]
    w_out_ref, init_ref, cited_ref, q_ref, wk_ref, wv_ref = refs[ways : ways + 6]
    lat_ref, ctx_ref = refs[ways + 6 : ways + 8]
    latents, mixed, bias = refs[ways + 8 : ways + 11]
    kb, hp = pl.program_id(0), pl.program_id(1)
    clips = KEYS // LAT
    half = LAT // 2

    @pl.when(hp == 0)
    def _():
        tails = []
        for k in range(ways):
            for g in range(clips):
                rows = slice(g * LAT, (g + 1) * LAT)
                mixed[rows, k * 256 : k * 256 + 128] = mix[k][g, 0:64]
                mixed[rows, k * 256 + 128 : (k + 1) * 256] = mix[k][g, 64:128]
                low = slice(g * LAT, g * LAT + half)
                high = slice(g * LAT + half, (g + 1) * LAT)
                at = slice(ways * 256 + k * 64, ways * 256 + (k + 1) * 64)
                mixed[low, at] = mix[k][g, 128:160, 0:64]
                mixed[high, at] = mix[k][g, 128:160, 64:128]
        init = init_ref[...].astype(f32)
        lat = matmul(mixed[...], w_out_ref[...])
        for g in range(clips):
            rows = slice(g * LAT, (g + 1) * LAT)
            latents[rows] = (lat[rows] + init).astype(bf16)
        lat_ref[...] = latents[...]
        flags = cited_ref.shape[1]
        row = lax.broadcasted_iota(jnp.int32, (flags, KEYS), 0)
        col = lax.broadcasted_iota(jnp.int32, (flags, KEYS), 1)
        first = (row - kb * clips) * LAT
        expand = jnp.where((col >= first) & (col < first + LAT), 1.0, 0.0).astype(bf16)
        bias[...] = (matmul(cited_ref[...], expand) - 1.0) * -masked_score

    key = matmul(latents[...], wk_ref[...]).astype(bf16)
    value = matmul(latents[...], wv_ref[...]).astype(bf16)
    inv = 1.0 / math.sqrt(HD)
    for h in range(2):
        cols = slice(h * HD, (h + 1) * HD)
        s = matmul_nt(q_ref[:, cols], key[:, cols]) * inv + bias[...]
        if blocks == 1:
            top = jnp.max(s, axis=1, keepdims=True)
            p = jnp.exp(s - top)
            total = jnp.sum(p, axis=1, keepdims=True)
            o = matmul(p.astype(bf16), value[:, cols])
            ctx_ref[:, cols] = (o / total).astype(bf16)
        else:
            acc, tops, totals = refs[ways + 11 :]
            at = hp * 2 + h
            first = kb == 0
            old_top = jnp.where(first, masked_score, tops[at])
            top = jnp.maximum(old_top, jnp.max(s, axis=1, keepdims=True))
            alpha = jnp.where(first, 0.0, jnp.exp(old_top - top))
            p = jnp.where(s > 0.5 * masked_score, jnp.exp(s - top), 0.0)
            total = alpha * jnp.where(first, 0.0, totals[at]) + jnp.sum(p, axis=1, keepdims=True)
            o = alpha * jnp.where(first, 0.0, acc[at])
            o = o + matmul(p.astype(bf16), value[:, cols])
            tops[at] = top
            totals[at] = total
            acc[at] = o

            @pl.when(kb == blocks - 1)
            def _():
                ctx_ref[:, cols] = (o / total).astype(bf16)


def exchange(x, ways):
    out = [x]
    for k in range(1, ways):
        low = k & -k
        top = 1 << (k.bit_length() - 1)
        source = out[k ^ low] if k != low else x
        del top
        out.append(lax.ppermute(source, "mp", [(i, i ^ low) for i in range(ways)]))
    return out


def body(
    patches,
    clip_of,
    owner_of,
    cites,
    latent_init,
    w_query,
    w_key,
    w_value,
    w_out,
    wx_key,
    wx_value,
    queries,
):
    groups = lax.axis_size("seq")
    ways = lax.axis_size("mp")
    clip_total = owner_of.shape[0]
    rows, wide = patches.shape
    width = w_query.shape[1]
    heads = width // RHD
    block = 256

    w_parts = exchange(w_out, ways)
    w_cat = jnp.concatenate([w[:256] for w in w_parts] + [w[256:] for w in w_parts], axis=0)

    whole = lambda shape: pl.BlockSpec(shape, lambda *_: (0,) * len(shape))
    chunk = min(8, clip_total)
    packed, lat_part = pl.pallas_call(
        partial_kernel,
        grid_spec=pltpu.PrefetchScalarGridSpec(
            num_scalar_prefetch=1,
            grid=(rows // block,),
            in_specs=[
                whole((1, rows)),
                pl.BlockSpec((block, wide), lambda i, *_: (i, 0)),
                whole((LAT, wide)),
                whole((wide, width)),
                whole((wide, width)),
                whole((wide, width)),
            ],
            out_specs=[whole((groups, LAT, 384)), whole((LAT, 384))],
            scratch_shapes=[
                pltpu.VMEM((heads * LAT, width), bf16),
                pltpu.VMEM((heads * LAT, rows), f32),
                pltpu.VMEM((heads, rows, RHD), bf16),
                pltpu.VMEM((heads, chunk * LAT, rows), bf16),
                pltpu.VMEM((clip_total, heads * LAT, 1), f32),
            ],
        ),
        out_shape=[
            jax.ShapeDtypeStruct((groups, LAT, 384), bf16),
            jax.ShapeDtypeStruct((LAT, 384), f32),
        ],
        name="partials",
    )(owner_of, clip_of.reshape(1, rows), patches, latent_init, w_query, w_key, w_value)

    got = lax.all_to_all(packed, "seq", split_axis=0, concat_axis=0, tiled=True)

    spread = pl.pallas_call(
        merge_kernel,
        out_shape=jax.ShapeDtypeStruct((groups, 160, 128), bf16),
        name="merge",
    )(got, lat_part)

    everyone = lax.all_to_all(spread, "seq", split_axis=0, concat_axis=0, tiled=True)
    mixes = exchange(everyone, ways)

    question_count = cites.shape[0]
    question_len = queries.shape[0] // question_count
    cite_hot = cites[:, :, None] == jnp.arange(clip_total, dtype=jnp.int32)[None, None, :]
    cite_owner = jnp.sum(cite_hot * owner_of[None, None, :], axis=2)
    flags = -(-groups // 128) * 128
    cited = jnp.any(
        cite_owner[:, :, None] == jnp.arange(flags, dtype=jnp.int32)[None, None, :], axis=1
    )
    token_cited = jnp.repeat(cited.astype(bf16), question_len, axis=0)

    tokens, cross = queries.shape
    blocks = groups * LAT // KEYS
    pair = 2 * HD
    per_pair = lambda shape: pl.BlockSpec(shape, lambda kb, hp: (0, hp))
    scratch = [
        pltpu.VMEM((KEYS, wide), bf16),
        pltpu.VMEM((KEYS, wide), bf16),
        pltpu.VMEM((tokens, KEYS), f32),
    ]
    if blocks > 1:
        scratch += [
            pltpu.VMEM((cross // HD, tokens, HD), f32),
            pltpu.VMEM((cross // HD, tokens, 1), f32),
            pltpu.VMEM((cross // HD, tokens, 1), f32),
        ]
    latents, context = pl.pallas_call(
        functools.partial(cross_kernel, blocks=blocks, ways=ways),
        grid=(blocks, cross // pair),
        in_specs=[pl.BlockSpec((KEYS // LAT, 160, 128), lambda kb, hp: (kb, 0, 0))] * ways
        + [
            whole((wide, wide)),
            whole((LAT, wide)),
            whole((tokens, flags)),
            per_pair((tokens, pair)),
            per_pair((wide, pair)),
            per_pair((wide, pair)),
        ],
        out_specs=[
            pl.BlockSpec((KEYS, wide), lambda kb, hp: (kb, 0)),
            per_pair((tokens, pair)),
        ],
        out_shape=[
            jax.ShapeDtypeStruct((groups * LAT, wide), bf16),
            jax.ShapeDtypeStruct((tokens, cross), bf16),
        ],
        scratch_shapes=scratch,
        name="cross",
    )(*mixes, w_cat, latent_init, token_cited, queries, wx_key, wx_value)
    resampled = lax.dynamic_slice_in_dim(latents, lax.axis_index("seq") * LAT, LAT, axis=0)
    return (resampled, context)


def solution(mesh):
    in_specs = (
        P("seq", None),
        P("seq", None),
        P(),
        P("seq", None),
        P(),
        P(None, "mp"),
        P(None, "mp"),
        P(None, "mp"),
        P("mp", None),
        P(None, "mp"),
        P(None, "mp"),
        P("seq", "mp"),
    )
    out_specs = (P("seq", None), P("seq", "mp"))
    return jax.shard_map(body, mesh=mesh, in_specs=in_specs, out_specs=out_specs, check_vma=False)
```

time: 118 us -> 86 us (0.73)
  Pallas kernels: 0 us -> 27.5 us
  matrix products: 26.3 us -> 0 us
  other arithmetic: 22.5 us -> 0.18 us
  local copies, waits for them, and re-layouts: 34.6 us -> 17.4 us
  waiting for transfers between devices: 11.3 us -> 17.3 us
    pallas_call x0 -> x3, Pallas kernels: none -> 27.5 us  [the longest x1 13.4 us: body(): pl.pallas_call(functools.partial(cross_kernel, blocks=blocks, ways=ways),...]
    dot_general x14 -> x0, matrix products: 26.3 us -> none  [the longest x1 3.57 us: body(): jnp.einsum('htk,khd->thd', p.astype(bf16), cross_values.reshape(-1, cross...]
    select_n x10 -> x0, other arithmetic: 11.2 us -> none  [gather_axis(): x = jnp.where(low, jnp.stack([x, other]), jnp.stack([other, x]))]
    all_to_all x1, waiting for transfers between devices: 1.59 us -> 10.3 us  [body(): got = lax.all_to_all(packed, 'seq', split_axis=0, concat_axis=0, tiled=True)]
    ppermute x7 -> x6, waiting for transfers between devices: 9.69 us -> 1.33 us  [exchange(): out.append(lax.ppermute(source, 'mp', [(i, i ^ low) for i in range(ways)]))]
    reduce_sum x6 -> x0, other arithmetic: 6.21 us -> none  [the longest x1 2.11 us: body(): total = jnp.sum(raised, axis=-1)]
    convert_element_type x6 -> x0, local copies, waits for them, and re-layouts: 5.85 us -> none  [the longest x2 3.39 us: body(): out.reshape(groups, LAT, heads * RHD).astype(bf16)]
    all_to_all x0 -> x1, waiting for transfers between devices: none -> 5.73 us  [body(): lax.all_to_all(spread, 'seq', split_axis=0, concat_axis=0, tiled=True)]
  transfers between devices with their start and end apart: 8 -> 8, of which waited for: 4 -> 3; matrix products, arithmetic and copies ran while one was open for 33% -> 17% of each run, Pallas kernels for 0% -> 17%
where the time goes in v2:
time: 86 us; the launch traced here: 85.2 us
  Pallas kernels  27.5 us (32%)
  starting transfers between devices  21.9 us (25%)
  local copies, waits for them, and re-layouts  17.4 us (20%)
  waiting for transfers between devices  17.3 us (20%)
    unnamed x24, local copies, waits for them, and re-layouts  13.9 us
    pallas_call x1, Pallas kernels, body(): pl.pallas_call(functools.partial(cross_kernel, blocks=blocks, ways=ways),...  13.4 us
    ppermute x6, starting transfers between devices, exchange(): out.append(lax.ppermute(source, 'mp', [(i, i ^ low) for i in range(ways)]))  12.3 us
    pallas_call x1, Pallas kernels, body(): pl.pallas_call(partial_kernel, grid_spec=pltpu.PrefetchScalarGridSpec(num...  11.7 us
    all_to_all x1, waiting for transfers between devices, body(): got = lax.all_to_all(packed, 'seq', split_axis=0, concat_axis=0, tiled=True)  10.3 us
    all_to_all x1, waiting for transfers between devices, body(): lax.all_to_all(spread, 'seq', split_axis=0, concat_axis=0, tiled=True)  5.73 us
    all_to_all x1, starting transfers between devices, body(): got = lax.all_to_all(packed, 'seq', split_axis=0, concat_axis=0, tiled=True)  5.53 us
    all_to_all x1, starting transfers between devices, body(): lax.all_to_all(spread, 'seq', split_axis=0, concat_axis=0, tiled=True)  4.12 us
  transfers between devices with their start and end apart: 8, of which 3 were waited for; matrix products, arithmetic and copies ran while one was open for 17% of the time, Pallas kernels for 17%

profile of v2, /device:TPU:1, one launch (start us, length us, event | category | flops | bytes accessed | tf_op | source)
XLA Modules:
  0.0 85.2 jit_solution(378432636729555935)
XLA Ops:
  0.6 2.1 %collective-permute-start.4 = (bf16[320,1280]{1,0:T(8,128)(2,1)}, bf16[320,1280]{1,0:T(8,128)(2,1)}, u32[]{:S(2)}, u32[]{:S(2)}) collective-permute-start(bf16[320,1280]{1,0:T(8,128)(2,1)} %param.20), channel_id=1, source_target_pairs={{0,2},{1,3},{2,0},{3,1},{4,6},{5,7},{6,4},{7,5},{8,10},{9,11},{10,... | collective-permute-start | bytes 2457608 | tf_op jit(solution)/shard_map/ppermute | solution.py:234
  2.8 1.0 %collective-permute-start.3 = (bf16[320,1280]{1,0:T(8,128)(2,1)}, bf16[320,1280]{1,0:T(8,128)(2,1)}, u32[]{:S(2)}, u32[]{:S(2)}) collective-permute-start(bf16[320,1280]{1,0:T(8,128)(2,1)} %param.20), channel_id=1, source_target_pairs={{0,1},{1,0},{2,3},{3,2},{4,5},{5,4},{6,7},{7,6},{8,9},{9,8},{10,11... | collective-permute-start | bytes 2457608 | tf_op jit(solution)/shard_map/ppermute | solution.py:234
  3.7 2.2 %copy.18.wq_ref = bf16[1280,320]{1,0:T(8,128)(2,1)} copy(bf16[1280,320]{0,1:T(8,128)(2,1)} %param.17) | data formatting | bytes 1638400 | tf_op args[5]
  5.9 2.2 %copy.19.wk_ref = bf16[1280,320]{1,0:T(8,128)(2,1)} copy(bf16[1280,320]{0,1:T(8,128)(2,1)} %param.18) | data formatting | bytes 1638400 | tf_op args[6]
  8.1 1.3 %copy.20.wv_ref = bf16[1280,320]{1,0:T(8,128)(2,1)} copy(bf16[1280,320]{0,1:T(8,128)(2,1)S(1)} %copy-done.1) | data formatting | bytes 1638400 | tf_op args[7]
  9.4 11.7 %partials.1 = (bf16[8,64,384]{2,1,0:T(8,128)(2,1)}, f32[64,384]{1,0:T(8,128)}) custom-call(s32[8]{0:T(128)} %owner_ref.1, s32[1,1024]{1,0:T(1,128)} %bitcast.3, bf16[1024,1280]{1,0:T(8,128)(2,1)} %patches_ref.1, bf16[64,1280]{1,0:T(8,128)(2,1)} %refs_5_.1, bf16[1280,320]{1,0:T(8,128)(2,1)} %copy.18.wq_ref, bf16[1280,320]{1,0:T(8,128)(2,1)} %copy.19.wk_ref, ...), custom_call_target="tpu_custom_call" | custom-call | tf_op jit(solution)/shard_map/partials/pallas_call | solution.py:265
  21.2 5.5 %all-to-all-start = ((bf16[8,64,384]{2,1,0:T(8,128)(2,1)}), bf16[8,64,384]{2,1,0:T(8,128)(2,1)}, u32[]{:S(2)}, u32[]{:S(2)}) async-start(bf16[8,64,384]{2,1,0:T(8,128)(2,1)} %get-tuple-element.6), calls=%async_computation | async-start | bytes 786432 | tf_op jit(solution)/shard_map/all_to_all | solution.py:294
  26.8 1.1 %slice_dynamic-update-slice_fusion.3 = bf16[1280,1280]{1,0:T(8,128)(2,1)S(1)} fusion(bf16[320,1280]{1,0:T(8,128)(2,1)} %param.20), kind=kLoop, calls=%fused_computation.3 | loop fusion | bytes 1310720
  27.9 10.3 %all-to-all-done.got_ref = bf16[8,64,384]{2,1,0:T(8,128)(2,1)} async-done(((bf16[8,64,384]{2,1,0:T(8,128)(2,1)}), bf16[8,64,384]{2,1,0:T(8,128)(2,1)}, u32[]{:S(2)}, u32[]{:S(2)}) %all-to-all-start) | async-done | bytes 393248 | tf_op jit(solution)/shard_map/all_to_all | solution.py:294
  38.2 2.4 %merge.1 = bf16[8,160,128]{2,1,0:T(8,128)(2,1)} custom-call(bf16[8,64,384]{2,1,0:T(8,128)(2,1)} %all-to-all-done.got_ref, f32[64,384]{1,0:T(8,128)} %get-tuple-element.7.lat_ref), custom_call_target="tpu_custom_call" | custom-call | tf_op jit(solution)/shard_map/merge/pallas_call | solution.py:296
  40.6 4.1 %all-to-all-start.1 = ((bf16[8,160,128]{2,1,0:T(8,128)(2,1)}), bf16[8,160,128]{2,1,0:T(8,128)(2,1)}, u32[]{:S(2)}, u32[]{:S(2)}) async-start(bf16[8,160,128]{2,1,0:T(8,128)(2,1)} %merge.1), calls=%async_computation.1 | async-start | bytes 655360 | tf_op jit(solution)/shard_map/all_to_all | solution.py:302
  44.8 1.3 %collective-permute-start.5 = (bf16[320,1280]{1,0:T(8,128)(2,1)}, bf16[320,1280]{1,0:T(8,128)(2,1)}, u32[]{:S(2)}, u32[]{:S(2)}) collective-permute-start(bf16[320,1280]{1,0:T(8,128)(2,1)} %collective-permute-done.4), channel_id=1, source_target_pairs={{0,1},{1,0},{2,3},{3,2},{4,5},{5,4},{6,7},{7,6},{8,9},{9,8},{10,11... | collective-permute-start | bytes 2457608 | tf_op jit(solution)/shard_map/ppermute | solution.py:234
  46.1 1.1 %slice_dynamic-update-slice_fusion.2 = bf16[1280,1280]{1,0:T(8,128)(2,1)S(1)} fusion(bf16[1280,1280]{1,0:T(8,128)(2,1)S(1)} %slice_dynamic-update-slice_fusion.3, bf16[320,1280]{1,0:T(8,128)(2,1)} %collective-permute-done.3), kind=kLoop, calls=%fused_computation.2 | loop fusion | bytes 1310720
  47.2 5.7 %all-to-all-done.1.refs_0_ = bf16[8,160,128]{2,1,0:T(8,128)(2,1)} async-done(((bf16[8,160,128]{2,1,0:T(8,128)(2,1)}), bf16[8,160,128]{2,1,0:T(8,128)(2,1)}, u32[]{:S(2)}, u32[]{:S(2)}) %all-to-all-start.1) | async-done | bytes 327712 | tf_op jit(solution)/shard_map/all_to_all | solution.py:302
  53.2 1.1 %slice_dynamic-update-slice_fusion.1 = bf16[1280,1280]{1,0:T(8,128)(2,1)S(1)} fusion(bf16[1280,1280]{1,0:T(8,128)(2,1)S(1)} %slice_dynamic-update-slice_fusion.2, bf16[320,1280]{1,0:T(8,128)(2,1)} %collective-permute-done.4), kind=kLoop, calls=%fused_computation.1 | loop fusion | bytes 1310720
  54.3 3.5 %collective-permute-start = (bf16[8,160,128]{2,1,0:T(8,128)(2,1)}, bf16[8,160,128]{2,1,0:T(8,128)(2,1)S(1)}, u32[]{:S(2)}, u32[]{:S(2)}) collective-permute-start(bf16[8,160,128]{2,1,0:T(8,128)(2,1)} %all-to-all-done.1.refs_0_), channel_id=1, source_target_pairs={{0,1},{1,0},{2,3},{3,2},{4,5},{5,4},{6,7},{7,6},{8,9},{9,8},{10,11... | collective-permute-start | bytes 983048 | tf_op jit(solution)/shard_map/ppermute | solution.py:234
  57.8 1.3 %collective-permute-done.1.refs_2_ = bf16[8,160,128]{2,1,0:T(8,128)(2,1)S(1)} collective-permute-done((bf16[8,160,128]{2,1,0:T(8,128)(2,1)}, bf16[8,160,128]{2,1,0:T(8,128)(2,1)S(1)}, u32[]{:S(2)}, u32[]{:S(2)}) %collective-permute-start.1) | collective-permute-done | bytes 327712 | tf_op jit(solution)/shard_map/ppermute | solution.py:234
  59.1 4.3 %collective-permute-start.2 = (bf16[8,160,128]{2,1,0:T(8,128)(2,1)S(1)}, bf16[8,160,128]{2,1,0:T(8,128)(2,1)S(1)}, u32[]{:S(2)}, u32[]{:S(2)}) collective-permute-start(bf16[8,160,128]{2,1,0:T(8,128)(2,1)S(1)} %collective-permute-done.1.refs_2_), channel_id=1, source_target_pairs={{0,1},{1,0},{2,3},{3,2},{4,5},{5,4},{6,7},{7,6},{8,9},{9,8},{10,11... | collective-permute-start | bytes 983048 | tf_op jit(solution)/shard_map/ppermute | solution.py:234
  63.4 1.1 %slice_dynamic-update-slice_fusion = bf16[1280,1280]{1,0:T(8,128)(2,1)S(1)} fusion(bf16[1280,1280]{1,0:T(8,128)(2,1)S(1)} %slice_dynamic-update-slice_fusion.1, bf16[320,1280]{1,0:T(8,128)(2,1)} %collective-permute-done.5), kind=kLoop, calls=%fused_computation | loop fusion | bytes 1310720
  64.5 0.9 %slice_dynamic-update-slice_fusion.7 = bf16[1280,1280]{1,0:T(8,128)(2,1)S(1)} fusion(bf16[1280,1280]{1,0:T(8,128)(2,1)S(1)} %slice_dynamic-update-slice_fusion, bf16[320,1280]{1,0:T(8,128)(2,1)} %param.20), kind=kLoop, calls=%fused_computation.7 | loop fusion | bytes 327680
  66.4 0.9 %slice_dynamic-update-slice_fusion.5 = bf16[1280,1280]{1,0:T(8,128)(2,1)S(1)} fusion(bf16[1280,1280]{1,0:T(8,128)(2,1)S(1)} %slice_dynamic-update-slice_fusion.6, bf16[320,1280]{1,0:T(8,128)(2,1)} %collective-permute-done.4), kind=kLoop, calls=%fused_computation.5 | loop fusion | bytes 327680
  69.1 1.1 %broadcast_in_dim.2 = bf16[32,16,128]{2,1,0:T(8,128)(2,1)} broadcast(bf16[32,128]{1,0:T(8,128)(2,1)S(1)} %convert_element_type.4), dimensions={0,2} | broadcast | bytes 139264 | tf_op jit(solution)/shard_map/broadcast_in_dim | solution.py:313
  70.2 13.4 %cross.1 = (bf16[512,1280]{1,0:T(8,128)(2,1)}, bf16[512,1024]{1,0:T(8,128)(2,1)}) custom-call(bf16[8,160,128]{2,1,0:T(8,128)(2,1)} %all-to-all-done.1.refs_0_, bf16[8,160,128]{2,1,0:T(8,128)(2,1)} %copy-done.3, bf16[8,160,128]{2,1,0:T(8,128)(2,1)} %copy-done.2, bf16[8,160,128]{2,1,0:T(8,128)(2,1)} %copy-done.4, bf16[1280,1280]{1,0:T(8,128)(2,1)} %copy-done, ...), custom_call_target="tpu_custom_call" | custom-call | tf_op jit(solution)/shard_map/cross/pallas_call | solution.py:330
  83.6 1.6 %constant_dynamic-slice_fusion = bf16[64,1280]{1,0:T(8,128)(2,1)} fusion(bf16[512,1280]{1,0:T(8,128)(2,1)} %get-tuple-element.8, s32[]{:T(128)S(6)} %select_n.3), kind=kLoop, calls=%fused_computation.12 | loop fusion | bytes 327684 | tf_op jit(solution)/shard_map/dynamic_slice | solution.py:353
  (25 shorter events, 3.1 us)
Async XLA Ops:
  0.6 7.5 %copy-start.1 = (bf16[1280,320]{0,1:T(8,128)(2,1)S(1)}, bf16[1280,320]{0,1:T(8,128)(2,1)}, u32[]{:S(2)}) copy-start(bf16[1280,320]{0,1:T(8,128)(2,1)} %param.19) | copy-start | bytes 2457604
  0.6 44.2 %collective-permute-start.4 = (bf16[320,1280]{1,0:T(8,128)(2,1)}, bf16[320,1280]{1,0:T(8,128)(2,1)}, u32[]{:S(2)}, u32[]{:S(2)}) collective-permute-start(bf16[320,1280]{1,0:T(8,128)(2,1)} %param.20), channel_id=1, source_target_pairs={{0,2},{1,3},{2,0},{3,1},{4,6},{5,7},{6,4},{7,5},{8,10},{9,11},{10,... | collective-permute-start | bytes 2457608 | tf_op jit(solution)/shard_map/ppermute | solution.py:234
  2.8 43.3 %collective-permute-start.3 = (bf16[320,1280]{1,0:T(8,128)(2,1)}, bf16[320,1280]{1,0:T(8,128)(2,1)}, u32[]{:S(2)}, u32[]{:S(2)}) collective-permute-start(bf16[320,1280]{1,0:T(8,128)(2,1)} %param.20), channel_id=1, source_target_pairs={{0,1},{1,0},{2,3},{3,2},{4,5},{5,4},{6,7},{7,6},{8,9},{9,8},{10,11... | collective-permute-start | bytes 2457608 | tf_op jit(solution)/shard_map/ppermute | solution.py:234
  9.4 17.3 %copy-start.5 = (s32[8]{0:T(128)S(1)}, s32[8]{0:T(128)}, u32[]{:S(2)}) copy-start(s32[8]{0:T(128)} %owner_ref.1) | copy-start | bytes 100
  9.4 17.3 %copy-start.6 = (s32[32,4]{0,1:T(4,128)S(1)}, s32[32,4]{0,1:T(4,128)}, u32[]{:S(2)}) copy-start(s32[32,4]{0,1:T(4,128)} %param.15) | copy-start | bytes 1540
  21.2 17.0 %all-to-all-start = ((bf16[8,64,384]{2,1,0:T(8,128)(2,1)}), bf16[8,64,384]{2,1,0:T(8,128)(2,1)}, u32[]{:S(2)}, u32[]{:S(2)}) async-start(bf16[8,64,384]{2,1,0:T(8,128)(2,1)} %get-tuple-element.6), calls=%async_computation | async-start | bytes 786432 | tf_op jit(solution)/shard_map/all_to_all | solution.py:294
  40.6 12.4 %all-to-all-start.1 = ((bf16[8,160,128]{2,1,0:T(8,128)(2,1)}), bf16[8,160,128]{2,1,0:T(8,128)(2,1)}, u32[]{:S(2)}, u32[]{:S(2)}) async-start(bf16[8,160,128]{2,1,0:T(8,128)(2,1)} %merge.1), calls=%async_computation.1 | async-start | bytes 655360 | tf_op jit(solution)/shard_map/all_to_all | solution.py:302
  44.8 18.5 %collective-permute-start.5 = (bf16[320,1280]{1,0:T(8,128)(2,1)}, bf16[320,1280]{1,0:T(8,128)(2,1)}, u32[]{:S(2)}, u32[]{:S(2)}) collective-permute-start(bf16[320,1280]{1,0:T(8,128)(2,1)} %collective-permute-done.4), channel_id=1, source_target_pairs={{0,1},{1,0},{2,3},{3,2},{4,5},{5,4},{6,7},{7,6},{8,9},{9,8},{10,11... | collective-permute-start | bytes 2457608 | tf_op jit(solution)/shard_map/ppermute | solution.py:234
  53.0 6.1 %collective-permute-start.1 = (bf16[8,160,128]{2,1,0:T(8,128)(2,1)}, bf16[8,160,128]{2,1,0:T(8,128)(2,1)S(1)}, u32[]{:S(2)}, u32[]{:S(2)}) collective-permute-start(bf16[8,160,128]{2,1,0:T(8,128)(2,1)} %all-to-all-done.1.refs_0_), channel_id=1, source_target_pairs={{0,2},{1,3},{2,0},{3,1},{4,6},{5,7},{6,4},{7,5},{8,10},{9,11},{10,... | collective-permute-start | bytes 983048 | tf_op jit(solution)/shard_map/ppermute | solution.py:234
  54.3 14.0 %collective-permute-start = (bf16[8,160,128]{2,1,0:T(8,128)(2,1)}, bf16[8,160,128]{2,1,0:T(8,128)(2,1)S(1)}, u32[]{:S(2)}, u32[]{:S(2)}) collective-permute-start(bf16[8,160,128]{2,1,0:T(8,128)(2,1)} %all-to-all-done.1.refs_0_), channel_id=1, source_target_pairs={{0,1},{1,0},{2,3},{3,2},{4,5},{5,4},{6,7},{7,6},{8,9},{9,8},{10,11... | collective-permute-start | bytes 983048 | tf_op jit(solution)/shard_map/ppermute | solution.py:234
  59.1 9.1 %copy-start.2 = (bf16[8,160,128]{2,1,0:T(8,128)(2,1)}, bf16[8,160,128]{2,1,0:T(8,128)(2,1)S(1)}, u32[]{:S(2)}) copy-start(bf16[8,160,128]{2,1,0:T(8,128)(2,1)S(1)} %collective-permute-done.1.refs_2_) | copy-start | bytes 983044
  59.1 9.2 %collective-permute-start.2 = (bf16[8,160,128]{2,1,0:T(8,128)(2,1)S(1)}, bf16[8,160,128]{2,1,0:T(8,128)(2,1)S(1)}, u32[]{:S(2)}, u32[]{:S(2)}) collective-permute-start(bf16[8,160,128]{2,1,0:T(8,128)(2,1)S(1)} %collective-permute-done.1.refs_2_), channel_id=1, source_target_pairs={{0,1},{1,0},{2,3},{3,2},{4,5},{5,4},{6,7},{7,6},{8,9},{9,8},{10,11... | collective-permute-start | bytes 983048 | tf_op jit(solution)/shard_map/ppermute | solution.py:234
  68.3 1.9 %copy-start = (bf16[1280,1280]{1,0:T(8,128)(2,1)}, bf16[1280,1280]{1,0:T(8,128)(2,1)S(1)}, u32[]{:S(2)}) copy-start(bf16[1280,1280]{1,0:T(8,128)(2,1)S(1)} %slice_dynamic-update-slice_fusion.4.refs_4_) | copy-start | bytes 9830404
  68.3 0.8 copy-start.3
  69.1 1.1 %copy-start.4 = (bf16[8,160,128]{2,1,0:T(8,128)(2,1)}, bf16[8,160,128]{2,1,0:T(8,128)(2,1)S(1)}, u32[]{:S(2)}) copy-start(bf16[8,160,128]{2,1,0:T(8,128)(2,1)S(1)} %collective-permute-done.2.refs_3_) | copy-start | bytes 983044

commit v3 on v2

v3 whole, which is shorter than its diff:
```python
import functools
import math

import jax
import jax.numpy as jnp
from jax import lax
from jax.experimental import pallas as pl
from jax.experimental.pallas import tpu as pltpu
from jax.sharding import PartitionSpec as P

RHD = 80
LAT = 64
HD = 128
KEYS = 512

masked_score = -1e30
f32 = jnp.float32
bf16 = jnp.bfloat16


def matmul(a, b):
    return jnp.dot(a, b, preferred_element_type=f32)


def matmul_nt(a, b):
    return lax.dot_general(a, b, (((1,), (1,)), ((), ())), preferred_element_type=f32)


def split3(x):
    a = x.astype(bf16).astype(f32)
    b = (x - a).astype(bf16).astype(f32)
    return a, b, x - a - b


def pack(cols):
    x = jnp.concatenate(cols, axis=1)
    half = LAT // 2
    third = jnp.concatenate([x[:half, 256:320], x[half:, 256:320]], axis=1)
    return jnp.concatenate([x[:, :128], x[:, 128:256], third], axis=0)


def partial_kernel(
    owner_ref, clip_ref, patches_ref, lat_ref, wq_ref, wk_ref, wv_ref,
    out_ref, lat_out_ref, qbd, scores, values, masked, peaks, totals, lses,
):
    step = pl.program_id(0)
    block = patches_ref.shape[0]
    width = wq_ref.shape[0]
    heads = width // RHD
    clips = owner_ref.shape[0]
    scale = 1.0 / math.sqrt(RHD)

    @pl.when(step == 0)
    def _():
        lat = lat_ref[...]
        q = matmul_nt(lat, wq_ref[...])
        lane = lax.broadcasted_iota(jnp.int32, q.shape, 1)
        for h in range(heads):
            inside = (lane >= h * RHD) & (lane < (h + 1) * RHD)
            qbd[h * LAT : (h + 1) * LAT, :] = jnp.where(inside, q, 0.0).astype(bf16)
        lk = matmul_nt(wk_ref[...], lat).astype(bf16)
        lv = matmul_nt(wv_ref[...], lat).astype(bf16)
        s = matmul(qbd[...], lk) * scale
        peak = jnp.max(s, axis=1, keepdims=True)
        p = jnp.exp(s - peak)
        total = jnp.sum(p, axis=1, keepdims=True)
        pb = p.astype(bf16)
        inv = 1.0 / total
        out = []
        for h in range(heads):
            rows = slice(h * LAT, (h + 1) * LAT)
            out.append(matmul_nt(pb[rows], lv[h * RHD : (h + 1) * RHD]) * inv[rows])
        lat_out_ref[0:160] = pack(out)
        lse = jnp.broadcast_to(peak + jnp.log(total), (heads * LAT, 128)).T[0:8]
        for i in range(heads * LAT // 128):
            lat_out_ref[160 + i : 161 + i] = lse[0:1, i * 128 : (i + 1) * 128]

    x = patches_ref[...]
    here = pl.ds(pl.multiple_of(step * block, block), block)
    kt = matmul_nt(wk_ref[...], x).astype(bf16)
    values[:, here] = matmul_nt(wv_ref[...], x).astype(bf16)
    scores[:, here] = matmul(qbd[...], kt) * scale

    @pl.when(step == pl.num_programs(0) - 1)
    def _():
        clip = clip_ref[...]
        group = masked.shape[1] // LAT
        rounds = clips // group
        tall = 16
        lane = lax.broadcasted_iota(jnp.int32, (tall, 128), 1)

        def peak_pass(rows):
            s = scores[rows, :]

            def one(base, carry):
                selected, stat = carry
                for k in range(group):
                    c = base * group + k
                    inside = clip == c
                    peak = jnp.max(jnp.where(inside, s, masked_score), axis=1, keepdims=True)
                    selected = jnp.where(inside, peak, selected)
                    stat = jnp.where(lane == c, peak, stat)
                return selected, stat

            init = (jnp.zeros(s.shape, f32), jnp.zeros((tall, 128), f32))
            if rounds == 1:
                selected, stat = one(0, init)
            else:
                selected, stat = lax.fori_loop(0, rounds, one, init)
            peaks[rows, :] = stat
            return jnp.exp(s - selected)

        def mask_pass(h, r, p, base, stat):
            pb = p.astype(bf16)
            for k in range(group):
                c = base * group + k
                inside = clip == c
                total = jnp.sum(jnp.where(inside, p, 0.0), axis=1, keepdims=True)
                stat = jnp.where(lane == c, total, stat)
                keep = jnp.where(inside, 1.0, 0.0).astype(bf16)
                masked[h, k * LAT + r * tall : k * LAT + (r + 1) * tall, :] = pb * keep
            return stat

        def rows_of(h, r):
            return slice(h * LAT + r * tall, h * LAT + (r + 1) * tall)

        def emit(base, outs):
            for k in range(group):
                c = base * group + k
                cols = []
                for h in range(heads):
                    t = totals[h * LAT : (h + 1) * LAT, :]
                    pick = lax.broadcasted_iota(jnp.int32, t.shape, 1) == c
                    t = jnp.sum(jnp.where(pick, t, 0.0), axis=1, keepdims=True)
                    inv = 1.0 / jnp.where(t > 0, t, 1.0)
                    cols.append(outs[h][k * LAT : (k + 1) * LAT] * inv)
                out_ref[owner_ref[c], 0:160, :] = pack(cols).astype(bf16)

        if rounds == 1:
            outs = []
            for h in range(heads):
                for r in range(LAT // tall):
                    rows = rows_of(h, r)
                    p = peak_pass(rows)
                    totals[rows, :] = mask_pass(h, r, p, 0, jnp.zeros((tall, 128), f32))
                outs.append(matmul_nt(masked[h], values[h * RHD : (h + 1) * RHD, :]))
            emit(0, outs)
        else:
            totals[...] = jnp.zeros(totals.shape, f32)
            for h in range(heads):
                for r in range(LAT // tall):
                    rows = rows_of(h, r)
                    scores[rows, :] = peak_pass(rows)

            def one_round(base, carry):
                outs = []
                for h in range(heads):
                    for r in range(LAT // tall):
                        rows = rows_of(h, r)
                        totals[rows, :] = mask_pass(h, r, scores[rows, :], base, totals[rows, :])
                    outs.append(matmul_nt(masked[h], values[h * RHD : (h + 1) * RHD, :]))
                emit(base, outs)
                return carry

            lax.fori_loop(0, rounds, one_round, 0)

        t = totals[...]
        live = t > 0
        lse = jnp.where(live, peaks[...] + jnp.log(jnp.where(live, t, 1.0)), masked_score)
        for i, part in enumerate(split3(lse.T)):
            lses[i] = part

        def tail(c, carry):
            rows = []
            for i in range(3):
                row = lses[i, pl.ds(c, 1), :]
                rows += [row[:, j * 128 : (j + 1) * 128] for j in range(heads * LAT // 128)]
            rows.append(jnp.zeros((16 - len(rows), 128), f32))
            out_ref[owner_ref[c], 160:176, :] = jnp.concatenate(rows, axis=0).astype(bf16)
            return carry

        if clips <= 8:
            for c in range(clips):
                tail(c, 0)
        else:
            lax.fori_loop(0, clips, tail, 0)


def merge_kernel(got_ref, lat_ref, out_ref):
    groups = got_ref.shape[0]
    lse = [lat_ref[160:162]]
    for g in range(groups):
        tail = got_ref[g, 160:176, :].astype(f32)
        lse.append(tail[0:2] + tail[2:4] + tail[4:6])
    best = functools.reduce(jnp.maximum, lse)
    weights = [jnp.exp(x - best) for x in lse]
    inv = 1.0 / sum(weights[1:], weights[0])
    rows = [w * inv for w in weights]
    short = -2 * len(rows) % 128
    table = jnp.concatenate(rows + [jnp.zeros((short, 128), f32)], axis=0).T
    lane = lax.broadcasted_iota(jnp.int32, (LAT, 128), 1)
    half = LAT // 2
    total = [0.0, 0.0, 0.0]
    for g in range(groups + 1):
        col = [
            table[(h % 2) * LAT : (h % 2 + 1) * LAT, 2 * g + h // 2 : 2 * g + h // 2 + 1]
            for h in range(4)
        ]
        factors = (
            jnp.where(lane < 80, col[0], col[1]),
            jnp.where(lane < 32, col[1], jnp.where(lane < 112, col[2], col[3])),
            jnp.where(lane[:half] < 64, col[3][:half], col[3][half:]),
        )
        for i, (lo, hi) in enumerate(((0, 64), (64, 128), (128, 160))):
            piece = lat_ref[lo:hi] if g == 0 else got_ref[g - 1, lo:hi, :].astype(f32)
            total[i] = total[i] + factors[i] * piece
    for i, (lo, hi) in enumerate(((0, 64), (64, 128), (128, 160))):
        piece = total[i].astype(bf16)
        for g in range(groups):
            out_ref[g, lo:hi, :] = piece


def cross_kernel(me_ref, *refs, blocks, ways):
    mix = refs[:ways]
    w_refs = refs[ways : 2 * ways]
    init_ref, cited_ref, q_ref, wk_ref, wv_ref = refs[2 * ways : 2 * ways + 5]
    lat_ref, ctx_ref = refs[2 * ways + 5 : 2 * ways + 7]
    latents, mixed, bias, w_all, sems = refs[2 * ways + 7 : 2 * ways + 12]
    kb, hp = pl.program_id(0), pl.program_id(1)
    clips = KEYS // LAT
    half = LAT // 2
    tokens = q_ref.shape[0]
    questions = cited_ref.shape[0]

    def copies():
        for k in range(ways):
            yield pltpu.make_async_copy(
                w_refs[k].at[0:256], w_all.at[k * 256 : (k + 1) * 256], sems.at[2 * k]
            )
            at = ways * 256 + k * 64
            yield pltpu.make_async_copy(
                w_refs[k].at[256:320], w_all.at[at : at + 64], sems.at[2 * k + 1]
            )

    @pl.when(hp == 0)
    def _():
        @pl.when(kb == 0)
        def _():
            for copy in copies():
                copy.start()

        for k in range(ways):
            for g in range(clips):
                rows = slice(g * LAT, (g + 1) * LAT)
                mixed[rows, k * 256 : k * 256 + 128] = mix[k][g, 0:64]
                mixed[rows, k * 256 + 128 : (k + 1) * 256] = mix[k][g, 64:128]
                low = slice(g * LAT, g * LAT + half)
                high = slice(g * LAT + half, (g + 1) * LAT)
                at = slice(ways * 256 + k * 64, ways * 256 + (k + 1) * 64)
                mixed[low, at] = mix[k][g, 128:160, 0:64]
                mixed[high, at] = mix[k][g, 128:160, 64:128]
        flags = cited_ref.shape[1]
        row = lax.broadcasted_iota(jnp.int32, (flags, KEYS), 0)
        col = lax.broadcasted_iota(jnp.int32, (flags, KEYS), 1)
        first = (row - kb * clips) * LAT
        expand = jnp.where((col >= first) & (col < first + LAT), 1.0, 0.0).astype(bf16)
        asked = matmul(cited_ref[...], expand).astype(bf16)
        row = lax.broadcasted_iota(jnp.int32, (tokens, questions), 0)
        first = lax.broadcasted_iota(jnp.int32, (tokens, questions), 1) * (tokens // questions)
        repeat = (row >= first) & (row < first + tokens // questions)
        repeat = jnp.where(repeat, 1.0, 0.0).astype(bf16)
        bias[...] = (matmul(repeat, asked) - 1.0) * -masked_score

        @pl.when(kb == 0)
        def _():
            for copy in copies():
                copy.wait()

        init = init_ref[...].astype(f32)
        lat = matmul(mixed[...], w_all[...])
        for g in range(clips):
            rows = slice(g * LAT, (g + 1) * LAT)
            latents[rows] = (lat[rows] + init).astype(bf16)
        me = me_ref[0]

        @pl.when(me // clips == kb)
        def _():
            lat_ref[...] = latents[pl.ds(pl.multiple_of(me % clips * LAT, LAT), LAT), :]

    key = matmul(latents[...], wk_ref[...]).astype(bf16)
    value = matmul(latents[...], wv_ref[...]).astype(bf16)
    inv = 1.0 / math.sqrt(HD)
    tall = min(128, tokens)
    for h in range(2):
        cols = slice(h * HD, (h + 1) * HD)
        for r in range(tokens // tall):
            rows = slice(r * tall, (r + 1) * tall)
            s = matmul_nt(q_ref[rows, cols], key[:, cols]) * inv + bias[rows]
            if blocks == 1:
                top = jnp.max(s, axis=1, keepdims=True)
                p = jnp.exp(s - top)
                total = jnp.sum(p, axis=1, keepdims=True)
                o = matmul(p.astype(bf16), value[:, cols])
                ctx_ref[rows, cols] = (o * (1.0 / total)).astype(bf16)
            else:
                acc, tops, totals = refs[2 * ways + 12 :]
                at = hp * 2 + h
                first = kb == 0
                old_top = jnp.where(first, masked_score, tops[at, rows])
                top = jnp.maximum(old_top, jnp.max(s, axis=1, keepdims=True))
                alpha = jnp.where(first, 0.0, jnp.exp(old_top - top))
                p = jnp.where(s > 0.5 * masked_score, jnp.exp(s - top), 0.0)
                total = jnp.where(first, 0.0, totals[at, rows]) * alpha
                total = total + jnp.sum(p, axis=1, keepdims=True)
                o = jnp.where(first, 0.0, acc[at, rows]) * alpha
                o = o + matmul(p.astype(bf16), value[:, cols])
                tops[at, rows] = top
                totals[at, rows] = total
                acc[at, rows] = o
                ctx_ref[rows, cols] = (o * (1.0 / jnp.maximum(total, 1e-30))).astype(bf16)


def exchange(x, ways):
    out = [x]
    for k in range(1, ways):
        low = k & -k
        source = out[k ^ low] if k != low else x
        out.append(lax.ppermute(source, "mp", [(i, i ^ low) for i in range(ways)]))
    return out


def body(
    patches,
    clip_of,
    owner_of,
    cites,
    latent_init,
    w_query,
    w_key,
    w_value,
    w_out,
    wx_key,
    wx_value,
    queries,
):
    groups = lax.axis_size("seq")
    ways = lax.axis_size("mp")
    clip_total = owner_of.shape[0]
    rows, wide = patches.shape
    width = w_query.shape[1]
    heads = width // RHD
    block = 256

    w_parts = exchange(w_out, ways)

    whole = lambda shape: pl.BlockSpec(shape, lambda *_: (0,) * len(shape))
    chunk = min(8, clip_total)
    packed, lat_part = pl.pallas_call(
        partial_kernel,
        grid_spec=pltpu.PrefetchScalarGridSpec(
            num_scalar_prefetch=1,
            grid=(rows // block,),
            in_specs=[
                whole((1, rows)),
                pl.BlockSpec((block, wide), lambda i, *_: (i, 0)),
                whole((LAT, wide)),
                whole((width, wide)),
                whole((width, wide)),
                whole((width, wide)),
            ],
            out_specs=[whole((groups, 176, 128)), whole((168, 128))],
            scratch_shapes=[
                pltpu.VMEM((heads * LAT, width), bf16),
                pltpu.VMEM((heads * LAT, rows), f32),
                pltpu.VMEM((width, rows), bf16),
                pltpu.VMEM((heads, chunk * LAT, rows), bf16),
                pltpu.VMEM((heads * LAT, 128), f32),
                pltpu.VMEM((heads * LAT, 128), f32),
                pltpu.VMEM((3, 128, heads * LAT), f32),
            ],
        ),
        out_shape=[
            jax.ShapeDtypeStruct((groups, 176, 128), bf16),
            jax.ShapeDtypeStruct((168, 128), f32),
        ],
        name="partials",
    )(owner_of, clip_of.reshape(1, rows), patches, latent_init, w_query.T, w_key.T, w_value.T)

    got = lax.all_to_all(packed, "seq", split_axis=0, concat_axis=0, tiled=True)

    spread = pl.pallas_call(
        merge_kernel,
        out_shape=jax.ShapeDtypeStruct((groups, 160, 128), bf16),
        name="merge",
    )(got, lat_part)

    everyone = lax.all_to_all(spread, "seq", split_axis=0, concat_axis=0, tiled=True)
    mixes = exchange(everyone, ways)

    cite_hot = cites[:, :, None] == jnp.arange(clip_total, dtype=jnp.int32)[None, None, :]
    cite_owner = jnp.sum(cite_hot * owner_of[None, None, :], axis=2)
    flags = -(-groups // 128) * 128
    cited = jnp.any(
        cite_owner[:, :, None] == jnp.arange(flags, dtype=jnp.int32)[None, None, :], axis=1
    ).astype(bf16)

    tokens, cross = queries.shape
    blocks = groups * LAT // KEYS
    pair = 2 * HD
    per_pair = lambda shape: pl.BlockSpec(shape, lambda kb, hp, *_: (0, hp))
    anywhere = pl.BlockSpec(memory_space=pl.ANY)
    scratch = [
        pltpu.VMEM((KEYS, wide), bf16),
        pltpu.VMEM((KEYS, wide), bf16),
        pltpu.VMEM((tokens, KEYS), f32),
        pltpu.VMEM((wide, wide), bf16),
        pltpu.SemaphoreType.DMA((2 * ways,)),
    ]
    if blocks > 1:
        scratch += [
            pltpu.VMEM((cross // HD, tokens, HD), f32),
            pltpu.VMEM((cross // HD, tokens, 1), f32),
            pltpu.VMEM((cross // HD, tokens, 1), f32),
        ]
    resampled, context = pl.pallas_call(
        functools.partial(cross_kernel, blocks=blocks, ways=ways),
        grid_spec=pltpu.PrefetchScalarGridSpec(
            num_scalar_prefetch=1,
            grid=(blocks, cross // pair),
            in_specs=[pl.BlockSpec((KEYS // LAT, 160, 128), lambda kb, hp, *_: (kb, 0, 0))] * ways
            + [anywhere] * ways
            + [
                whole((LAT, wide)),
                whole(cited.shape),
                per_pair((tokens, pair)),
                per_pair((wide, pair)),
                per_pair((wide, pair)),
            ],
            out_specs=[whole((LAT, wide)), per_pair((tokens, pair))],
            scratch_shapes=scratch,
        ),
        out_shape=[
            jax.ShapeDtypeStruct((LAT, wide), bf16),
            jax.ShapeDtypeStruct((tokens, cross), bf16),
        ],
        name="cross",
    )(
        lax.axis_index("seq").astype(jnp.int32).reshape(1),
        *mixes,
        *w_parts,
        latent_init,
        cited,
        queries,
        wx_key,
        wx_value,
    )
    return (resampled, context)


def solution(mesh):
    in_specs = (
        P("seq", None),
        P("seq", None),
        P(),
        P("seq", None),
        P(),
        P(None, "mp"),
        P(None, "mp"),
        P(None, "mp"),
        P("mp", None),
        P(None, "mp"),
        P(None, "mp"),
        P("seq", "mp"),
    )
    out_specs = (P("seq", None), P("seq", "mp"))
    return jax.shard_map(body, mesh=mesh, in_specs=in_specs, out_specs=out_specs, check_vma=False)
```

time: 86 us -> 76 us (0.88)
  local copies, waits for them, and re-layouts: 17.4 us -> 1.18 us
  Pallas kernels: 27.5 us -> 33.2 us
  starting transfers between devices: 21.9 us -> 25.2 us
  waiting for transfers between devices: 17.3 us -> 14.5 us
    unnamed x24 -> x18, local copies, waits for them, and re-layouts: 13.9 us -> 1.18 us
    pallas_call x1, Pallas kernels: 13.4 us -> 19.2 us  [body(): pl.pallas_call(functools.partial(cross_kernel, blocks=blocks, ways=ways),...]
    all_to_all x1, waiting for transfers between devices: 10.3 us -> 7.42 us  [body(): got = lax.all_to_all(packed, 'seq', split_axis=0, concat_axis=0, tiled=True)]
    dynamic_slice x1 -> x0, local copies, waits for them, and re-layouts: 1.59 us -> none  [body(): lax.dynamic_slice_in_dim(latents, lax.axis_index('seq') * LAT, LAT, axis=0)]
    all_to_all x1, starting transfers between devices: 4.12 us -> 5.71 us  [body(): lax.all_to_all(spread, 'seq', split_axis=0, concat_axis=0, tiled=True)]
    broadcast_in_dim x1 -> x0, local copies, waits for them, and re-layouts: 1.06 us -> none  [body(): token_cited = jnp.repeat(cited.astype(bf16), question_len, axis=0)]
    concatenate x1 -> x0, local copies, waits for them, and re-layouts: 0.93 us -> none  [body(): jnp.concatenate([w[:256] for w in w_parts] + [w[256:] for w in w_parts],...]
    ppermute x6, starting transfers between devices: 12.3 us -> 13.2 us  [exchange(): out.append(lax.ppermute(source, 'mp', [(i, i ^ low) for i in range(ways)]))]
  transfers between devices with their start and end apart: 8 -> 8, of which waited for: 3 -> 5; matrix products, arithmetic and copies ran while one was open for 17% -> 1% of each run, Pallas kernels for 17% -> 3%
where the time goes in v3:
time: 76 us; the launch traced here: 75.6 us
  Pallas kernels  33.2 us (44%)
  starting transfers between devices  25.2 us (33%)
  waiting for transfers between devices  14.5 us (19%)
  local copies, waits for them, and re-layouts  1.18 us (2%)
  other arithmetic  0.77 us (1%)
    pallas_call x1, Pallas kernels, body(): pl.pallas_call(functools.partial(cross_kernel, blocks=blocks, ways=ways),...  19.2 us
    ppermute x6, starting transfers between devices, exchange(): out.append(lax.ppermute(source, 'mp', [(i, i ^ low) for i in range(ways)]))  13.2 us
    pallas_call x1, Pallas kernels, body(): pl.pallas_call(partial_kernel, grid_spec=pltpu.PrefetchScalarGridSpec(num...  11.7 us
    all_to_all x1, waiting for transfers between devices, body(): got = lax.all_to_all(packed, 'seq', split_axis=0, concat_axis=0, tiled=True)  7.42 us
    all_to_all x1, starting transfers between devices, body(): got = lax.all_to_all(packed, 'seq', split_axis=0, concat_axis=0, tiled=True)  6.34 us
    all_to_all x1, starting transfers between devices, body(): lax.all_to_all(spread, 'seq', split_axis=0, concat_axis=0, tiled=True)  5.71 us
    all_to_all x1, waiting for transfers between devices, body(): lax.all_to_all(spread, 'seq', split_axis=0, concat_axis=0, tiled=True)  4.86 us
    pallas_call x1, Pallas kernels, body(): pl.pallas_call(merge_kernel, out_shape=jax.ShapeDtypeStruct((groups, 160,...  2.29 us
  transfers between devices with their start and end apart: 8, of which 5 were waited for; matrix products, arithmetic and copies ran while one was open for 1% of the time, Pallas kernels for 3%

profile of v3, /device:TPU:1, one launch (start us, length us, event | category | flops | bytes accessed | tf_op | source)
XLA Modules:
  0.0 75.6 jit_solution(2840646213543933784)
XLA Ops:
  0.6 0.0 copy-start.2
  0.7 11.7 %partials.1 = (bf16[8,176,128]{2,1,0:T(8,128)(2,1)}, f32[168,128]{1,0:T(8,128)}) custom-call(s32[8]{0:T(128)} %owner_ref.1, s32[1,1024]{1,0:T(1,128)} %bitcast.8, bf16[1024,1280]{1,0:T(8,128)(2,1)} %patches_ref.1, bf16[64,1280]{1,0:T(8,128)(2,1)} %refs_8_.1, bf16[320,1280]{1,0:T(8,128)(2,1)} %bitcast.5, bf16[320,1280]{1,0:T(8,128)(2,1)} %bitcast.6, ...), custom_call_target="tpu_custom_call" | custom-call | tf_op jit(solution)/shard_map/partials/pallas_call | solution.py:358
  12.4 6.3 %all-to-all-start = ((bf16[8,176,128]{2,1,0:T(8,128)(2,1)}), bf16[8,176,128]{2,1,0:T(8,128)(2,1)S(1)}, u32[]{:S(2)}, u32[]{:S(2)}) async-start(bf16[8,176,128]{2,1,0:T(8,128)(2,1)} %get-tuple-element.4), calls=%async_computation | async-start | bytes 720896 | tf_op jit(solution)/shard_map/all_to_all | solution.py:389
  18.7 1.3 %collective-permute-start.4 = (bf16[320,1280]{1,0:T(8,128)(2,1)S(1)}, bf16[320,1280]{1,0:T(8,128)(2,1)S(1)}, u32[]{:S(2)}, u32[]{:S(2)}) collective-permute-start(bf16[320,1280]{1,0:T(8,128)(2,1)S(1)} %copy-done.2), channel_id=1, source_target_pairs={{0,2},{1,3},{2,0},{3,1},{4,6},{5,7},{6,4},{7,5},{8,10},{9,11},{10,... | collective-permute-start | bytes 2457608 | tf_op jit(solution)/shard_map/ppermute | solution.py:328
  20.0 7.4 %all-to-all-done.got_ref = bf16[8,176,128]{2,1,0:T(8,128)(2,1)S(1)} async-done(((bf16[8,176,128]{2,1,0:T(8,128)(2,1)}), bf16[8,176,128]{2,1,0:T(8,128)(2,1)S(1)}, u32[]{:S(2)}, u32[]{:S(2)}) %all-to-all-start) | async-done | bytes 360480 | tf_op jit(solution)/shard_map/all_to_all | solution.py:389
  27.5 0.7 copy-done
  28.2 2.3 %merge.1 = bf16[8,160,128]{2,1,0:T(8,128)(2,1)} custom-call(bf16[8,176,128]{2,1,0:T(8,128)(2,1)} %copy-done, f32[168,128]{1,0:T(8,128)} %get-tuple-element.5.lat_ref), custom_call_target="tpu_custom_call" | custom-call | tf_op jit(solution)/shard_map/merge/pallas_call | solution.py:391
  30.5 5.7 %all-to-all-start.1 = ((bf16[8,160,128]{2,1,0:T(8,128)(2,1)}), bf16[8,160,128]{2,1,0:T(8,128)(2,1)S(1)}, u32[]{:S(2)}, u32[]{:S(2)}) async-start(bf16[8,160,128]{2,1,0:T(8,128)(2,1)} %merge.1), calls=%async_computation.1 | async-start | bytes 655360 | tf_op jit(solution)/shard_map/all_to_all | solution.py:397
  36.2 1.1 %collective-permute-start.3 = (bf16[320,1280]{1,0:T(8,128)(2,1)S(1)}, bf16[320,1280]{1,0:T(8,128)(2,1)S(1)}, u32[]{:S(2)}, u32[]{:S(2)}) collective-permute-start(bf16[320,1280]{1,0:T(8,128)(2,1)S(1)} %copy-done.2), channel_id=1, source_target_pairs={{0,1},{1,0},{2,3},{3,2},{4,5},{5,4},{6,7},{7,6},{8,9},{9,8},{10,11... | collective-permute-start | bytes 2457608 | tf_op jit(solution)/shard_map/ppermute | solution.py:328
  37.3 0.3 collective-permute-done.4.refs_6_
  37.6 1.8 %collective-permute-start.5 = (bf16[320,1280]{1,0:T(8,128)(2,1)S(1)}, bf16[320,1280]{1,0:T(8,128)(2,1)}, u32[]{:S(2)}, u32[]{:S(2)}) collective-permute-start(bf16[320,1280]{1,0:T(8,128)(2,1)S(1)} %collective-permute-done.4.refs_6_), channel_id=1, source_target_pairs={{0,1},{1,0},{2,3},{3,2},{4,5},{5,4},{6,7},{7,6},{8,9},{9,8},{10,11... | collective-permute-start | bytes 2457608 | tf_op jit(solution)/shard_map/ppermute | solution.py:328
  39.5 4.9 %all-to-all-done.1.refs_0_ = bf16[8,160,128]{2,1,0:T(8,128)(2,1)S(1)} async-done(((bf16[8,160,128]{2,1,0:T(8,128)(2,1)}), bf16[8,160,128]{2,1,0:T(8,128)(2,1)S(1)}, u32[]{:S(2)}, u32[]{:S(2)}) %all-to-all-start.1) | async-done | bytes 327712 | tf_op jit(solution)/shard_map/all_to_all | solution.py:397
  44.3 1.2 %collective-permute-start.1 = (bf16[8,160,128]{2,1,0:T(8,128)(2,1)S(1)}, bf16[8,160,128]{2,1,0:T(8,128)(2,1)S(1)}, u32[]{:S(2)}, u32[]{:S(2)}) collective-permute-start(bf16[8,160,128]{2,1,0:T(8,128)(2,1)S(1)} %all-to-all-done.1.refs_0_), channel_id=1, source_target_pairs={{0,2},{1,3},{2,0},{3,1},{4,6},{5,7},{6,4},{7,5},{8,10},{9,11},{10,... | collective-permute-start | bytes 983048 | tf_op jit(solution)/shard_map/ppermute | solution.py:328
  45.6 3.4 %collective-permute-start = (bf16[8,160,128]{2,1,0:T(8,128)(2,1)S(1)}, bf16[8,160,128]{2,1,0:T(8,128)(2,1)S(1)}, u32[]{:S(2)}, u32[]{:S(2)}) collective-permute-start(bf16[8,160,128]{2,1,0:T(8,128)(2,1)S(1)} %all-to-all-done.1.refs_0_), channel_id=1, source_target_pairs={{0,1},{1,0},{2,3},{3,2},{4,5},{5,4},{6,7},{7,6},{8,9},{9,8},{10,11... | collective-permute-start | bytes 983048 | tf_op jit(solution)/shard_map/ppermute | solution.py:328
  49.0 1.3 %collective-permute-done.1.refs_2_ = bf16[8,160,128]{2,1,0:T(8,128)(2,1)S(1)} collective-permute-done((bf16[8,160,128]{2,1,0:T(8,128)(2,1)S(1)}, bf16[8,160,128]{2,1,0:T(8,128)(2,1)S(1)}, u32[]{:S(2)}, u32[]{:S(2)}) %collective-permute-start.1) | collective-permute-done | bytes 327712 | tf_op jit(solution)/shard_map/ppermute | solution.py:328
  50.2 4.3 %collective-permute-start.2 = (bf16[8,160,128]{2,1,0:T(8,128)(2,1)S(1)}, bf16[8,160,128]{2,1,0:T(8,128)(2,1)}, u32[]{:S(2)}, u32[]{:S(2)}) collective-permute-start(bf16[8,160,128]{2,1,0:T(8,128)(2,1)S(1)} %collective-permute-done.1.refs_2_), channel_id=1, source_target_pairs={{0,1},{1,0},{2,3},{3,2},{4,5},{5,4},{6,7},{7,6},{8,9},{9,8},{10,11... | collective-permute-start | bytes 983048 | tf_op jit(solution)/shard_map/ppermute | solution.py:328
  54.5 0.1 select_reduce_fusion
  54.6 0.1 fusion
  54.7 0.6 convert_element_type.4.refs_9_
  55.3 0.0 collective-permute-done.3.refs_5_
  55.4 0.6 collective-permute-done.2.refs_3_
  55.9 0.3 copy-done.4
  56.2 0.1 copy-done.6
  56.4 19.2 %cross.1 = (bf16[64,1280]{1,0:T(8,128)(2,1)}, bf16[512,1024]{1,0:T(8,128)(2,1)}) custom-call(s32[1]{0:T(128)} %bitcast.me_ref, bf16[8,160,128]{2,1,0:T(8,128)(2,1)} %copy-done.1, bf16[8,160,128]{2,1,0:T(8,128)(2,1)} %copy-done.6, bf16[8,160,128]{2,1,0:T(8,128)(2,1)} %copy-done.5, bf16[8,160,128]{2,1,0:T(8,128)(2,1)} %collective-permute-done.2.refs_3_, ...), custom_call_target="tpu_custom_call" | custom-call | tf_op jit(solution)/shard_map/cross/pallas_call | solution.py:425
  (16 shorter events, 0.0 us)
Async XLA Ops:
  0.6 18.1 %copy-start.2 = (bf16[320,1280]{1,0:T(8,128)(2,1)S(1)}, bf16[320,1280]{1,0:T(8,128)(2,1)}, u32[]{:S(2)}) copy-start(bf16[320,1280]{1,0:T(8,128)(2,1)} %refs_4_.1) | copy-start | bytes 2457604
  0.6 53.9 %copy-start.7 = (s32[8]{0:T(128)S(1)}, s32[8]{0:T(128)}, u32[]{:S(2)}) copy-start(s32[8]{0:T(128)} %owner_ref.1) | copy-start | bytes 100
  0.7 53.9 %copy-start.8 = (s32[32,4]{0,1:T(4,128)S(1)}, s32[32,4]{0,1:T(4,128)}, u32[]{:S(2)}) copy-start(s32[32,4]{0,1:T(4,128)} %param.15) | copy-start | bytes 1540
  12.4 15.1 %all-to-all-start = ((bf16[8,176,128]{2,1,0:T(8,128)(2,1)}), bf16[8,176,128]{2,1,0:T(8,128)(2,1)S(1)}, u32[]{:S(2)}, u32[]{:S(2)}) async-start(bf16[8,176,128]{2,1,0:T(8,128)(2,1)} %get-tuple-element.4), calls=%async_computation | async-start | bytes 720896 | tf_op jit(solution)/shard_map/all_to_all | solution.py:389
  18.7 18.9 %collective-permute-start.4 = (bf16[320,1280]{1,0:T(8,128)(2,1)S(1)}, bf16[320,1280]{1,0:T(8,128)(2,1)S(1)}, u32[]{:S(2)}, u32[]{:S(2)}) collective-permute-start(bf16[320,1280]{1,0:T(8,128)(2,1)S(1)} %copy-done.2), channel_id=1, source_target_pairs={{0,2},{1,3},{2,0},{3,1},{4,6},{5,7},{6,4},{7,5},{8,10},{9,11},{10,... | collective-permute-start | bytes 2457608 | tf_op jit(solution)/shard_map/ppermute | solution.py:328
  27.5 0.7 copy-start
  30.5 13.8 %all-to-all-start.1 = ((bf16[8,160,128]{2,1,0:T(8,128)(2,1)}), bf16[8,160,128]{2,1,0:T(8,128)(2,1)S(1)}, u32[]{:S(2)}, u32[]{:S(2)}) async-start(bf16[8,160,128]{2,1,0:T(8,128)(2,1)} %merge.1), calls=%async_computation.1 | async-start | bytes 655360 | tf_op jit(solution)/shard_map/all_to_all | solution.py:397
  36.2 19.1 %collective-permute-start.3 = (bf16[320,1280]{1,0:T(8,128)(2,1)S(1)}, bf16[320,1280]{1,0:T(8,128)(2,1)S(1)}, u32[]{:S(2)}, u32[]{:S(2)}) collective-permute-start(bf16[320,1280]{1,0:T(8,128)(2,1)S(1)} %copy-done.2), channel_id=1, source_target_pairs={{0,1},{1,0},{2,3},{3,2},{4,5},{5,4},{6,7},{7,6},{8,9},{9,8},{10,11... | collective-permute-start | bytes 2457608 | tf_op jit(solution)/shard_map/ppermute | solution.py:328
  37.6 18.3 %copy-start.3 = (bf16[320,1280]{1,0:T(8,128)(2,1)}, bf16[320,1280]{1,0:T(8,128)(2,1)S(1)}, u32[]{:S(2)}) copy-start(bf16[320,1280]{1,0:T(8,128)(2,1)S(1)} %collective-permute-done.4.refs_6_) | copy-start | bytes 2457604
  37.6 17.7 %collective-permute-start.5 = (bf16[320,1280]{1,0:T(8,128)(2,1)S(1)}, bf16[320,1280]{1,0:T(8,128)(2,1)}, u32[]{:S(2)}, u32[]{:S(2)}) collective-permute-start(bf16[320,1280]{1,0:T(8,128)(2,1)S(1)} %collective-permute-done.4.refs_6_), channel_id=1, source_target_pairs={{0,1},{1,0},{2,3},{3,2},{4,5},{5,4},{6,7},{7,6},{8,9},{9,8},{10,11... | collective-permute-start | bytes 2457608 | tf_op jit(solution)/shard_map/ppermute | solution.py:328
  44.3 11.6 %copy-start.1 = (bf16[8,160,128]{2,1,0:T(8,128)(2,1)}, bf16[8,160,128]{2,1,0:T(8,128)(2,1)S(1)}, u32[]{:S(2)}) copy-start(bf16[8,160,128]{2,1,0:T(8,128)(2,1)S(1)} %all-to-all-done.1.refs_0_) | copy-start | bytes 983044
  44.3 5.9 %collective-permute-start.1 = (bf16[8,160,128]{2,1,0:T(8,128)(2,1)S(1)}, bf16[8,160,128]{2,1,0:T(8,128)(2,1)S(1)}, u32[]{:S(2)}, u32[]{:S(2)}) collective-permute-start(bf16[8,160,128]{2,1,0:T(8,128)(2,1)S(1)} %all-to-all-done.1.refs_0_), channel_id=1, source_target_pairs={{0,2},{1,3},{2,0},{3,1},{4,6},{5,7},{6,4},{7,5},{8,10},{9,11},{10,... | collective-permute-start | bytes 983048 | tf_op jit(solution)/shard_map/ppermute | solution.py:328
  45.6 9.8 %collective-permute-start = (bf16[8,160,128]{2,1,0:T(8,128)(2,1)S(1)}, bf16[8,160,128]{2,1,0:T(8,128)(2,1)S(1)}, u32[]{:S(2)}, u32[]{:S(2)}) collective-permute-start(bf16[8,160,128]{2,1,0:T(8,128)(2,1)S(1)} %all-to-all-done.1.refs_0_), channel_id=1, source_target_pairs={{0,1},{1,0},{2,3},{3,2},{4,5},{5,4},{6,7},{7,6},{8,9},{9,8},{10,11... | collective-permute-start | bytes 983048 | tf_op jit(solution)/shard_map/ppermute | solution.py:328
  50.2 5.7 %copy-start.5 = (bf16[8,160,128]{2,1,0:T(8,128)(2,1)}, bf16[8,160,128]{2,1,0:T(8,128)(2,1)S(1)}, u32[]{:S(2)}) copy-start(bf16[8,160,128]{2,1,0:T(8,128)(2,1)S(1)} %collective-permute-done.1.refs_2_) | copy-start | bytes 983044
  50.2 5.7 %collective-permute-start.2 = (bf16[8,160,128]{2,1,0:T(8,128)(2,1)S(1)}, bf16[8,160,128]{2,1,0:T(8,128)(2,1)}, u32[]{:S(2)}, u32[]{:S(2)}) collective-permute-start(bf16[8,160,128]{2,1,0:T(8,128)(2,1)S(1)} %collective-permute-done.1.refs_2_), channel_id=1, source_target_pairs={{0,1},{1,0},{2,3},{3,2},{4,5},{5,4},{6,7},{7,6},{8,9},{9,8},{10,11... | collective-permute-start | bytes 983048 | tf_op jit(solution)/shard_map/ppermute | solution.py:328
  55.3 0.9 %copy-start.4 = (bf16[320,1280]{1,0:T(8,128)(2,1)}, bf16[320,1280]{1,0:T(8,128)(2,1)S(1)}, u32[]{:S(2)}) copy-start(bf16[320,1280]{1,0:T(8,128)(2,1)S(1)} %collective-permute-done.3.refs_5_) | copy-start | bytes 2457604
  55.3 1.0 %copy-start.6 = (bf16[8,160,128]{2,1,0:T(8,128)(2,1)}, bf16[8,160,128]{2,1,0:T(8,128)(2,1)S(1)}, u32[]{:S(2)}) copy-start(bf16[8,160,128]{2,1,0:T(8,128)(2,1)S(1)} %collective-permute-done.refs_1_) | copy-start | bytes 983044

commit v4 on v3

v4 whole, which is shorter than its diff:
```python
import functools
import math

import jax
import jax.numpy as jnp
from jax import lax
from jax.experimental import pallas as pl
from jax.experimental.pallas import tpu as pltpu
from jax.sharding import PartitionSpec as P

RHD = 80
LAT = 64
HD = 128
KEYS = 512

masked_score = -1e30
f32 = jnp.float32
bf16 = jnp.bfloat16


def matmul(a, b):
    return jnp.dot(a, b, preferred_element_type=f32)


def matmul_nt(a, b):
    return lax.dot_general(a, b, (((1,), (1,)), ((), ())), preferred_element_type=f32)


def split3(x):
    a = x.astype(bf16).astype(f32)
    b = (x - a).astype(bf16).astype(f32)
    return a, b, x - a - b


def pack(cols):
    x = jnp.concatenate(cols, axis=1)
    half = LAT // 2
    third = jnp.concatenate([x[:half, 256:320], x[half:, 256:320]], axis=1)
    return jnp.concatenate([x[:, :128], x[:, 128:256], third], axis=0)


def head_mask(q):
    lane = lax.broadcasted_iota(jnp.int32, q.shape, 1)
    heads = q.shape[1] // RHD
    return [
        jnp.where((lane >= h * RHD) & (lane < (h + 1) * RHD), q, 0.0).astype(bf16)
        for h in range(heads)
    ]


def partial_kernel(
    owner_ref, clip_ref, lat_ref, patches_hbm, wq_hbm, wk_hbm, wv_hbm,
    out_ref, query_ref, patches, wq_ref, wk_ref, wv_ref, sems,
    scores, values, masked, peaks, totals, lses,
):
    pieces = sems.shape[0] - 3
    block = patches.shape[0] // pieces
    width = wq_ref.shape[0]
    heads = width // RHD
    clips = owner_ref.shape[0]
    scale = 1.0 / math.sqrt(RHD)

    def patch_copy(i):
        rows = slice(i * block, (i + 1) * block)
        return pltpu.make_async_copy(patches_hbm.at[rows], patches.at[rows], sems.at[3 + i])

    fetch_q = pltpu.make_async_copy(wq_hbm, wq_ref, sems.at[0])
    fetch_k = pltpu.make_async_copy(wk_hbm, wk_ref, sems.at[1])
    fetch_v = pltpu.make_async_copy(wv_hbm, wv_ref, sems.at[2])
    fetch_q.start()
    fetch_k.start()
    patch_copy(0).start()
    fetch_v.start()
    for i in range(1, pieces):
        patch_copy(i).start()
    fetch_q.wait()
    for h, rows in enumerate(head_mask(matmul_nt(lat_ref[...], wq_ref[...]))):
        query_ref[h * LAT : (h + 1) * LAT, :] = rows
    fetch_k.wait()
    for i in range(pieces):
        here = slice(i * block, (i + 1) * block)
        patch_copy(i).wait()
        x = patches[here, :]
        kt = matmul_nt(wk_ref[...], x).astype(bf16)
        scores[:, here] = matmul(query_ref[...], kt) * scale
        if i == 0:
            fetch_v.wait()
        values[:, here] = matmul_nt(wv_ref[...], x).astype(bf16)

    clip = clip_ref[...]
    group = masked.shape[1] // LAT
    rounds = clips // group
    tall = 16
    lane = lax.broadcasted_iota(jnp.int32, (tall, 128), 1)

    def peak_pass(rows):
        s = scores[rows, :]

        def one(base, carry):
            selected, stat = carry
            for k in range(group):
                c = base * group + k
                inside = clip == c
                peak = jnp.max(jnp.where(inside, s, masked_score), axis=1, keepdims=True)
                selected = jnp.where(inside, peak, selected)
                stat = jnp.where(lane == c, peak, stat)
            return selected, stat

        init = (jnp.zeros(s.shape, f32), jnp.zeros((tall, 128), f32))
        if rounds == 1:
            selected, stat = one(0, init)
        else:
            selected, stat = lax.fori_loop(0, rounds, one, init)
        peaks[rows, :] = stat
        return jnp.exp(s - selected)

    def mask_pass(h, r, p, base, stat):
        pb = p.astype(bf16)
        for k in range(group):
            c = base * group + k
            inside = clip == c
            total = jnp.sum(jnp.where(inside, p, 0.0), axis=1, keepdims=True)
            stat = jnp.where(lane == c, total, stat)
            keep = jnp.where(inside, 1.0, 0.0).astype(bf16)
            masked[h, k * LAT + r * tall : k * LAT + (r + 1) * tall, :] = pb * keep
        return stat

    def rows_of(h, r):
        return slice(h * LAT + r * tall, h * LAT + (r + 1) * tall)

    def emit(base, outs):
        for k in range(group):
            c = base * group + k
            cols = []
            for h in range(heads):
                t = totals[h * LAT : (h + 1) * LAT, :]
                pick = lax.broadcasted_iota(jnp.int32, t.shape, 1) == c
                t = jnp.sum(jnp.where(pick, t, 0.0), axis=1, keepdims=True)
                inv = 1.0 / jnp.where(t > 0, t, 1.0)
                cols.append(outs[h][k * LAT : (k + 1) * LAT] * inv)
            out_ref[owner_ref[c], 0:160, :] = pack(cols).astype(bf16)

    if rounds == 1:
        outs = []
        for h in range(heads):
            for r in range(LAT // tall):
                rows = rows_of(h, r)
                p = peak_pass(rows)
                totals[rows, :] = mask_pass(h, r, p, 0, jnp.zeros((tall, 128), f32))
            outs.append(matmul_nt(masked[h], values[h * RHD : (h + 1) * RHD, :]))
        emit(0, outs)
    else:
        totals[...] = jnp.zeros(totals.shape, f32)
        for h in range(heads):
            for r in range(LAT // tall):
                rows = rows_of(h, r)
                scores[rows, :] = peak_pass(rows)

        def one_round(base, carry):
            outs = []
            for h in range(heads):
                for r in range(LAT // tall):
                    rows = rows_of(h, r)
                    totals[rows, :] = mask_pass(h, r, scores[rows, :], base, totals[rows, :])
                outs.append(matmul_nt(masked[h], values[h * RHD : (h + 1) * RHD, :]))
            emit(base, outs)
            return carry

        lax.fori_loop(0, rounds, one_round, 0)

    t = totals[...]
    live = t > 0
    lse = jnp.where(live, peaks[...] + jnp.log(jnp.where(live, t, 1.0)), masked_score)
    for i, part in enumerate(split3(lse.T)):
        lses[i] = part

    def tail(c, carry):
        rows = []
        for i in range(3):
            row = lses[i, pl.ds(c, 1), :]
            rows += [row[:, j * 128 : (j + 1) * 128] for j in range(heads * LAT // 128)]
        rows.append(jnp.zeros((16 - len(rows), 128), f32))
        out_ref[owner_ref[c], 160:176, :] = jnp.concatenate(rows, axis=0).astype(bf16)
        return carry

    if clips <= 8:
        for c in range(clips):
            tail(c, 0)
    else:
        lax.fori_loop(0, clips, tail, 0)


def latent_kernel(lat_ref, query_ref, wk_ref, wv_ref, out_ref):
    heads = wk_ref.shape[0] // RHD
    lat = lat_ref[...]
    lk = matmul_nt(wk_ref[...], lat).astype(bf16)
    lv = matmul_nt(wv_ref[...], lat).astype(bf16)
    s = matmul(query_ref[...], lk) * (1.0 / math.sqrt(RHD))
    peak = jnp.max(s, axis=1, keepdims=True)
    p = jnp.exp(s - peak)
    total = jnp.sum(p, axis=1, keepdims=True)
    pb = p.astype(bf16)
    inv = 1.0 / total
    out = []
    for h in range(heads):
        rows = slice(h * LAT, (h + 1) * LAT)
        out.append(matmul_nt(pb[rows], lv[h * RHD : (h + 1) * RHD]) * inv[rows])
    out_ref[0:160] = pack(out)
    lse = jnp.broadcast_to(peak + jnp.log(total), (heads * LAT, 128)).T[0:8]
    for i in range(heads * LAT // 128):
        out_ref[160 + i : 161 + i] = lse[0:1, i * 128 : (i + 1) * 128]


def merge_kernel(got_ref, lat_ref, out_ref):
    groups = got_ref.shape[0]
    lse = [lat_ref[160:162]]
    for g in range(groups):
        tail = got_ref[g, 160:176, :].astype(f32)
        lse.append(tail[0:2] + tail[2:4] + tail[4:6])
    best = functools.reduce(jnp.maximum, lse)
    weights = [jnp.exp(x - best) for x in lse]
    inv = 1.0 / sum(weights[1:], weights[0])
    rows = [w * inv for w in weights]
    short = -2 * len(rows) % 128
    table = jnp.concatenate(rows + [jnp.zeros((short, 128), f32)], axis=0).T
    lane = lax.broadcasted_iota(jnp.int32, (LAT, 128), 1)
    half = LAT // 2
    total = [0.0, 0.0, 0.0]
    for g in range(groups + 1):
        col = [
            table[(h % 2) * LAT : (h % 2 + 1) * LAT, 2 * g + h // 2 : 2 * g + h // 2 + 1]
            for h in range(4)
        ]
        factors = (
            jnp.where(lane < 80, col[0], col[1]),
            jnp.where(lane < 32, col[1], jnp.where(lane < 112, col[2], col[3])),
            jnp.where(lane[:half] < 64, col[3][:half], col[3][half:]),
        )
        for i, (lo, hi) in enumerate(((0, 64), (64, 128), (128, 160))):
            piece = lat_ref[lo:hi] if g == 0 else got_ref[g - 1, lo:hi, :].astype(f32)
            total[i] = total[i] + factors[i] * piece
    for i, (lo, hi) in enumerate(((0, 64), (64, 128), (128, 160))):
        piece = total[i].astype(bf16)
        for g in range(groups):
            out_ref[g, lo:hi, :] = piece


def project(mixes, ways):
    clips = KEYS // LAT
    half = LAT // 2
    total = None
    for i in range(0, len(mixes), 2):
        folded = []
        for mix, w in zip(mixes[i : i + 2], ways[i : i + 2]):
            x = jnp.concatenate(
                [mix[:, 0:64].reshape(KEYS, 128), mix[:, 64:128].reshape(KEYS, 128)], axis=1
            )
            part = matmul(x, w[0:256])
            total = part if total is None else total + part
            folded.append(mix[:, 128:160])
        low = jnp.concatenate([t[:, :, 0:64] for t in folded], axis=2)
        high = jnp.concatenate([t[:, :, 64:128] for t in folded], axis=2)
        x = jnp.concatenate([low, high], axis=1).reshape(KEYS, 128)
        total = total + matmul(x, jnp.concatenate([w[256:320] for w in ways[i : i + 2]], axis=0))
    return total


def begin_kernel(a_ref, b_ref, wa_ref, wb_ref, init_ref, out_ref):
    init = init_ref[...].astype(f32)
    part = project([a_ref[...], b_ref[...]], [wa_ref[...], wb_ref[...]])
    for g in range(KEYS // LAT):
        rows = slice(g * LAT, (g + 1) * LAT)
        out_ref[rows] = part[rows] + init


def cross_kernel(me_ref, *refs, blocks, ways):
    mix = refs[:ways]
    w_refs = refs[ways : 2 * ways]
    init_ref, cited_ref, q_ref, wk_ref, wv_ref = refs[2 * ways : 2 * ways + 5]
    lat_ref, ctx_ref = refs[2 * ways + 5 : 2 * ways + 7]
    latents, bias, keys, vals, scores, weights = refs[2 * ways + 7 : 2 * ways + 13]
    clips = KEYS // LAT
    tokens = q_ref.shape[0]
    questions = cited_ref.shape[0]
    heads = q_ref.shape[1] // HD
    inv = 1.0 / math.sqrt(HD)
    tall = min(32, tokens)
    me = me_ref[0]

    def one_block(kb, carry):
        flags = cited_ref.shape[1]
        row = lax.broadcasted_iota(jnp.int32, (flags, KEYS), 0)
        col = lax.broadcasted_iota(jnp.int32, (flags, KEYS), 1)
        first = (row - kb * clips) * LAT
        expand = jnp.where((col >= first) & (col < first + LAT), 1.0, 0.0).astype(bf16)
        asked = matmul(cited_ref[...], expand).astype(bf16)
        row = lax.broadcasted_iota(jnp.int32, (tokens, questions), 0)
        first = lax.broadcasted_iota(jnp.int32, (tokens, questions), 1) * (tokens // questions)
        repeat = (row >= first) & (row < first + tokens // questions)
        repeat = jnp.where(repeat, 1.0, 0.0).astype(bf16)
        bias[...] = (matmul(repeat, asked) - 1.0) * -masked_score

        here = pl.ds(kb * clips, clips)
        part = project([m[here] for m in mix], [w[...] for w in w_refs])
        if init_ref.shape[0] == KEYS:
            latents[...] = (part + init_ref[...]).astype(bf16)
        else:
            init = init_ref[...].astype(f32)
            for g in range(clips):
                rows = slice(g * LAT, (g + 1) * LAT)
                latents[rows] = (part[rows] + init).astype(bf16)

        @pl.when(me // clips == kb)
        def _():
            lat_ref[...] = latents[pl.ds(pl.multiple_of(me % clips * LAT, LAT), LAT), :]

        for h in range(heads):
            cols = slice(h * HD, (h + 1) * HD)
            if h % 2 == 0:
                pair = slice(h * HD, (h + 2) * HD)
                keys[:, pair] = matmul(latents[...], wk_ref[:, pair]).astype(bf16)
                vals[:, pair] = matmul(latents[...], wv_ref[:, pair]).astype(bf16)
            slot = h % scores.shape[0]
            scores[slot] = matmul_nt(q_ref[:, cols], keys[:, cols])
            if blocks > 1:
                acc, tops, totals = refs[2 * ways + 13 :]
            sums = []
            for r in range(tokens // tall):
                rows = slice(r * tall, (r + 1) * tall)
                s = scores[slot, rows] * inv + bias[rows]
                top = jnp.max(s, axis=1, keepdims=True)
                if blocks > 1:
                    old = jnp.where(kb == 0, masked_score, tops[h, rows])
                    top = jnp.maximum(old, top)
                    tops[h, rows] = top
                    alpha = jnp.where(kb == 0, 0.0, jnp.exp(old - top))
                    p = jnp.where(s > 0.5 * masked_score, jnp.exp(s - top), 0.0)
                    total = alpha * jnp.where(kb == 0, 0.0, totals[h, rows])
                    totals[h, rows] = total + jnp.sum(p, axis=1, keepdims=True)
                    acc[h, rows] = alpha * jnp.where(kb == 0, 0.0, acc[h, rows])
                else:
                    p = jnp.exp(s - top)
                    sums.append(jnp.sum(p, axis=1, keepdims=True))
                weights[slot, rows] = p.astype(bf16)
            o = matmul(weights[slot], vals[:, cols])
            if blocks > 1:
                acc[h] = acc[h] + o
                ctx_ref[:, cols] = (acc[h] * (1.0 / jnp.maximum(totals[h], 1e-30))).astype(bf16)
            else:
                for r in range(tokens // tall):
                    rows = slice(r * tall, (r + 1) * tall)
                    ctx_ref[rows, cols] = (o[rows] * (1.0 / sums[r])).astype(bf16)
        return carry

    if blocks == 1:
        one_block(0, 0)
    else:
        lax.fori_loop(0, blocks, one_block, 0)


def exchange(x, ways):
    out = [x]
    for k in range(1, ways):
        low = k & -k
        source = out[k ^ low] if k != low else x
        out.append(lax.ppermute(source, "mp", [(i, i ^ low) for i in range(ways)]))
    return out


def body(
    patches,
    clip_of,
    owner_of,
    cites,
    latent_init,
    w_query,
    w_key,
    w_value,
    w_out,
    wx_key,
    wx_value,
    queries,
):
    groups = lax.axis_size("seq")
    ways = lax.axis_size("mp")
    clip_total = owner_of.shape[0]
    rows, wide = patches.shape
    width = w_query.shape[1]
    heads = width // RHD

    w_parts = exchange(w_out, ways)

    vmem = pl.BlockSpec(memory_space=pltpu.VMEM)
    smem = pl.BlockSpec(memory_space=pltpu.SMEM)
    anywhere = pl.BlockSpec(memory_space=pl.ANY)
    limit = lambda mib: pltpu.CompilerParams(vmem_limit_bytes=mib << 20)
    chunk = min(8, clip_total)
    pieces = 4
    wq, wk, wv = w_query.T, w_key.T, w_value.T
    packed, query_rows = pl.pallas_call(
        partial_kernel,
        in_specs=[smem, vmem, vmem] + [pl.BlockSpec(memory_space=pltpu.HBM)] * 4,
        out_specs=[vmem, vmem],
        scratch_shapes=[
            pltpu.VMEM((rows, wide), bf16),
            pltpu.VMEM((width, wide), bf16),
            pltpu.VMEM((width, wide), bf16),
            pltpu.VMEM((width, wide), bf16),
            pltpu.SemaphoreType.DMA((3 + pieces,)),
            pltpu.VMEM((heads * LAT, rows), f32),
            pltpu.VMEM((width, rows), bf16),
            pltpu.VMEM((heads, chunk * LAT, rows), bf16),
            pltpu.VMEM((heads * LAT, 128), f32),
            pltpu.VMEM((heads * LAT, 128), f32),
            pltpu.VMEM((3, 128, heads * LAT), f32),
        ],
        out_shape=[
            jax.ShapeDtypeStruct((groups, 176, 128), bf16),
            jax.ShapeDtypeStruct((heads * LAT, width), bf16),
        ],
        compiler_params=limit(32),
        name="partials",
    )(owner_of, clip_of.reshape(1, rows), latent_init, patches, wq, wk, wv)

    got = lax.all_to_all(packed, "seq", split_axis=0, concat_axis=0, tiled=True)

    lat_part = pl.pallas_call(
        latent_kernel,
        in_specs=[vmem] * 4,
        out_specs=vmem,
        out_shape=jax.ShapeDtypeStruct((168, 128), f32),
        compiler_params=limit(8),
        name="latents",
    )(latent_init, query_rows, wk, wv)

    spread = pl.pallas_call(
        merge_kernel,
        in_specs=[vmem] * 2,
        out_specs=vmem,
        out_shape=jax.ShapeDtypeStruct((groups, 160, 128), bf16),
        compiler_params=limit(16),
        name="merge",
    )(got, lat_part)

    everyone = lax.all_to_all(spread, "seq", split_axis=0, concat_axis=0, tiled=True)
    mixes = exchange(everyone, ways)

    cite_hot = cites[:, :, None] == jnp.arange(clip_total, dtype=jnp.int32)[None, None, :]
    cite_owner = jnp.sum(cite_hot * owner_of[None, None, :], axis=2)
    flags = -(-groups // 128) * 128
    cited = jnp.any(
        cite_owner[:, :, None] == jnp.arange(flags, dtype=jnp.int32)[None, None, :], axis=1
    ).astype(bf16)

    tokens, cross = queries.shape
    blocks = groups * LAT // KEYS
    scratch = [
        pltpu.VMEM((KEYS, wide), bf16),
        pltpu.VMEM((tokens, KEYS), f32),
        pltpu.VMEM((KEYS, cross), bf16),
        pltpu.VMEM((KEYS, cross), bf16),
        pltpu.VMEM((2, tokens, KEYS), f32),
        pltpu.VMEM((2, tokens, KEYS), bf16),
    ]
    init = latent_init
    if blocks == 1 and ways == 4 and KEYS > LAT:
        init = pl.pallas_call(
            begin_kernel,
            in_specs=[vmem] * 5,
            out_specs=vmem,
            out_shape=pltpu.VMEM((KEYS, wide), f32),
            compiler_params=limit(16),
            name="begin",
        )(mixes[0], mixes[1], w_parts[0], w_parts[1], latent_init)
        mixes, w_parts = mixes[2:], w_parts[2:]
    if blocks > 1:
        scratch += [
            pltpu.VMEM((cross // HD, tokens, HD), f32),
            pltpu.VMEM((cross // HD, tokens, 1), f32),
            pltpu.VMEM((cross // HD, tokens, 1), f32),
        ]
    resampled, context = pl.pallas_call(
        functools.partial(cross_kernel, blocks=blocks, ways=len(mixes)),
        in_specs=[smem] + [vmem] * (2 * len(mixes) + 5),
        out_specs=[vmem] * 2,
        scratch_shapes=scratch,
        out_shape=[
            jax.ShapeDtypeStruct((LAT, wide), bf16),
            jax.ShapeDtypeStruct((tokens, cross), bf16),
        ],
        compiler_params=limit(28),
        name="cross",
    )(
        lax.axis_index("seq").astype(jnp.int32).reshape(1),
        *mixes,
        *w_parts,
        init,
        cited,
        queries,
        wx_key,
        wx_value,
    )
    return (resampled, context)


def solution(mesh):
    in_specs = (
        P("seq", None),
        P("seq", None),
        P(),
        P("seq", None),
        P(),
        P(None, "mp"),
        P(None, "mp"),
        P(None, "mp"),
        P("mp", None),
        P(None, "mp"),
        P(None, "mp"),
        P("seq", "mp"),
    )
    out_specs = (P("seq", None), P("seq", "mp"))
    return jax.shard_map(body, mesh=mesh, in_specs=in_specs, out_specs=out_specs, check_vma=False)
```

time: 76 us -> 75.2 us (0.989)
  local copies, waits for them, and re-layouts: 1.18 us -> 9.19 us
  Pallas kernels: 33.2 us -> 26.4 us
  waiting for transfers between devices: 14.5 us -> 12.7 us
    unnamed x18 -> x30, local copies, waits for them, and re-layouts: 1.18 us -> 9.19 us
    pallas_call x3 -> x5, Pallas kernels: 33.2 us -> 26.4 us  [the longest x1 10.8 us: body(): pl.pallas_call(functools.partial(cross_kernel, blocks=blocks, ways=len(mi...]
    all_to_all x1, waiting for transfers between devices: 4.86 us -> 2.87 us  [body(): lax.all_to_all(spread, 'seq', split_axis=0, concat_axis=0, tiled=True)]
    ppermute x6, waiting for transfers between devices: 2.16 us -> 3.49 us  [exchange(): out.append(lax.ppermute(source, 'mp', [(i, i ^ low) for i in range(ways)]))]
    all_to_all x1, waiting for transfers between devices: 7.42 us -> 6.37 us  [body(): got = lax.all_to_all(packed, 'seq', split_axis=0, concat_axis=0, tiled=True)]
  transfers between devices with their start and end apart: 8 -> 8, of which waited for: 5 -> 4; matrix products, arithmetic and copies ran while one was open for 1% -> 0% of each run, Pallas kernels for 3% -> 7%
where the time goes in v4:
time: 75.2 us; the launch traced here: 74.5 us
  Pallas kernels  26.4 us (35%)
  starting transfers between devices  25.3 us (34%)
  waiting for transfers between devices  12.7 us (17%)
  local copies, waits for them, and re-layouts  9.19 us (12%)
  between operations  0.78 us (1%)
    ppermute x6, starting transfers between devices, exchange(): out.append(lax.ppermute(source, 'mp', [(i, i ^ low) for i in range(ways)]))  13.2 us
    pallas_call x1, Pallas kernels, body(): pl.pallas_call(functools.partial(cross_kernel, blocks=blocks, ways=len(mi...  10.8 us
    pallas_call x1, Pallas kernels, body(): pl.pallas_call(partial_kernel, in_specs=[smem, vmem, vmem] + [pl.BlockSpe...  10.4 us
    unnamed x30, local copies, waits for them, and re-layouts  9.19 us
    all_to_all x1, waiting for transfers between devices, body(): got = lax.all_to_all(packed, 'seq', split_axis=0, concat_axis=0, tiled=True)  6.37 us
    all_to_all x1, starting transfers between devices, body(): got = lax.all_to_all(packed, 'seq', split_axis=0, concat_axis=0, tiled=True)  6.36 us
    all_to_all x1, starting transfers between devices, body(): lax.all_to_all(spread, 'seq', split_axis=0, concat_axis=0, tiled=True)  5.71 us
    ppermute x6, waiting for transfers between devices, exchange(): out.append(lax.ppermute(source, 'mp', [(i, i ^ low) for i in range(ways)]))  3.49 us
  transfers between devices with their start and end apart: 8, of which 4 were waited for; matrix products, arithmetic and copies ran while one was open for 0% of the time, Pallas kernels for 7%

profile of v4, /device:TPU:1, one launch (start us, length us, event | category | flops | bytes accessed | tf_op | source)
XLA Modules:
  0.0 74.5 jit_solution(13735702958584562435)
XLA Ops:
  0.6 1.1 %copy-done = bf16[1280,320]{0,1:T(8,128)(2,1)S(1)} copy-done((bf16[1280,320]{0,1:T(8,128)(2,1)S(1)}, bf16[1280,320]{0,1:T(8,128)(2,1)}, u32[]{:S(2)}) %copy-start) | copy-done | bytes 819224
  1.8 1.1 %copy-done.2 = bf16[1280,320]{0,1:T(8,128)(2,1)S(1)} copy-done((bf16[1280,320]{0,1:T(8,128)(2,1)S(1)}, bf16[1280,320]{0,1:T(8,128)(2,1)}, u32[]{:S(2)}) %copy-start.2) | copy-done | bytes 819224
  2.9 1.7 %copy-done.4 = bf16[1024,1280]{1,0:T(8,128)(2,1)S(1)} copy-done((bf16[1024,1280]{1,0:T(8,128)(2,1)S(1)}, bf16[1024,1280]{1,0:T(8,128)(2,1)}, u32[]{:S(2)}) %copy-start.4) | copy-done | bytes 2621464
  4.7 0.9 %copy-done.7 = bf16[64,1280]{1,0:T(8,128)(2,1)S(1)} copy-done((bf16[64,1280]{1,0:T(8,128)(2,1)S(1)}, bf16[64,1280]{1,0:T(8,128)(2,1)}, u32[]{:S(2)}) %copy-start.7) | copy-done | bytes 163864
  5.6 1.1 %copy-done.10 = bf16[1280,320]{0,1:T(8,128)(2,1)S(1)} copy-done((bf16[1280,320]{0,1:T(8,128)(2,1)S(1)}, bf16[1280,320]{0,1:T(8,128)(2,1)}, u32[]{:S(2)}) %copy-start.10) | copy-done | bytes 819224
  6.7 0.7 copy-done.11
  8.1 10.4 %partials.1 = (bf16[8,176,128]{2,1,0:T(8,128)(2,1)}, bf16[256,320]{1,0:T(8,128)(2,1)S(1)}) custom-call(s32[8]{0:T(128)S(1)} %copy-done.12, s32[1,1024]{1,0:T(1,128)S(1)} %bitcast.10, bf16[64,1280]{1,0:T(8,128)(2,1)S(1)} %copy-done.7, bf16[1024,1280]{1,0:T(8,128)(2,1)S(1)} %copy-done.4, bf16[320,1280]{1,0:T(8,128)(2,1)S(1)} %bitcast.9, ...), custom_call_target="tpu_custom_call" | custom-call | tf_op jit(solution)/shard_map/partials/pallas_call | solution.py:400
  18.5 6.4 %all-to-all-start = ((bf16[8,176,128]{2,1,0:T(8,128)(2,1)}), bf16[8,176,128]{2,1,0:T(8,128)(2,1)S(1)}, u32[]{:S(2)}, u32[]{:S(2)}) async-start(bf16[8,176,128]{2,1,0:T(8,128)(2,1)} %get-tuple-element.4), calls=%async_computation | async-start | bytes 720896 | tf_op jit(solution)/shard_map/all_to_all | solution.py:425
  24.9 1.2 %collective-permute-start.2 = (bf16[320,1280]{1,0:T(8,128)(2,1)}, bf16[320,1280]{1,0:T(8,128)(2,1)}, u32[]{:S(2)}, u32[]{:S(2)}) collective-permute-start(bf16[320,1280]{1,0:T(8,128)(2,1)} %wa_ref.1), channel_id=1, source_target_pairs={{0,2},{1,3},{2,0},{3,1},{4,6},{5,7},{6,4},{7,5},{8,10},{9,11},{10,... | collective-permute-start | bytes 2457608 | tf_op jit(solution)/shard_map/ppermute | solution.py:366
  26.1 1.1 %latents.1.lat_ref = f32[168,128]{1,0:T(8,128)S(1)} custom-call(bf16[64,1280]{1,0:T(8,128)(2,1)S(1)} %copy-done.8, bf16[256,320]{1,0:T(8,128)(2,1)S(1)} %get-tuple-element.5.query_ref, bf16[320,1280]{1,0:T(8,128)(2,1)S(1)} %bitcast.6, bf16[320,1280]{1,0:T(8,128)(2,1)S(1)} %bitcast.8), custom_call_target="tpu_custom_call" | custom-call | tf_op jit(solution)/shard_map/latents/pallas_call | solution.py:427
  27.2 6.4 %all-to-all-done.got_ref = bf16[8,176,128]{2,1,0:T(8,128)(2,1)S(1)} async-done(((bf16[8,176,128]{2,1,0:T(8,128)(2,1)}), bf16[8,176,128]{2,1,0:T(8,128)(2,1)S(1)}, u32[]{:S(2)}, u32[]{:S(2)}) %all-to-all-start) | async-done | bytes 360480 | tf_op jit(solution)/shard_map/all_to_all | solution.py:425
  33.6 1.3 %merge.1 = bf16[8,160,128]{2,1,0:T(8,128)(2,1)} custom-call(bf16[8,176,128]{2,1,0:T(8,128)(2,1)S(1)} %all-to-all-done.got_ref, f32[168,128]{1,0:T(8,128)S(1)} %latents.1.lat_ref), custom_call_target="tpu_custom_call" | custom-call | tf_op jit(solution)/shard_map/merge/pallas_call | solution.py:436
  34.9 5.7 %all-to-all-start.1 = ((bf16[8,160,128]{2,1,0:T(8,128)(2,1)}), bf16[8,160,128]{2,1,0:T(8,128)(2,1)S(1)}, u32[]{:S(2)}, u32[]{:S(2)}) async-start(bf16[8,160,128]{2,1,0:T(8,128)(2,1)} %merge.1), calls=%async_computation.1 | async-start | bytes 655360 | tf_op jit(solution)/shard_map/all_to_all | solution.py:445
  40.6 1.2 %collective-permute-start.5 = (bf16[320,1280]{1,0:T(8,128)(2,1)}, bf16[320,1280]{1,0:T(8,128)(2,1)}, u32[]{:S(2)}, u32[]{:S(2)}) collective-permute-start(bf16[320,1280]{1,0:T(8,128)(2,1)} %wa_ref.1), channel_id=1, source_target_pairs={{0,1},{1,0},{2,3},{3,2},{4,5},{5,4},{6,7},{7,6},{8,9},{9,8},{10,11... | collective-permute-start | bytes 2457608 | tf_op jit(solution)/shard_map/ppermute | solution.py:366
  41.8 2.2 %collective-permute-done.2.refs_2_ = bf16[320,1280]{1,0:T(8,128)(2,1)} collective-permute-done((bf16[320,1280]{1,0:T(8,128)(2,1)}, bf16[320,1280]{1,0:T(8,128)(2,1)}, u32[]{:S(2)}, u32[]{:S(2)}) %collective-permute-start.2) | collective-permute-done | bytes 819232 | tf_op jit(solution)/shard_map/ppermute | solution.py:366
  44.0 1.8 %collective-permute-start.3 = (bf16[320,1280]{1,0:T(8,128)(2,1)}, bf16[320,1280]{1,0:T(8,128)(2,1)}, u32[]{:S(2)}, u32[]{:S(2)}) collective-permute-start(bf16[320,1280]{1,0:T(8,128)(2,1)} %collective-permute-done.2.refs_2_), channel_id=1, source_target_pairs={{0,1},{1,0},{2,3},{3,2},{4,5},{5,4},{6,7},{7,6},{8,9},{9,8},{10,11... | collective-permute-start | bytes 2457608 | tf_op jit(solution)/shard_map/ppermute | solution.py:366
  45.8 2.9 %all-to-all-done.1.a_ref = bf16[8,160,128]{2,1,0:T(8,128)(2,1)S(1)} async-done(((bf16[8,160,128]{2,1,0:T(8,128)(2,1)}), bf16[8,160,128]{2,1,0:T(8,128)(2,1)S(1)}, u32[]{:S(2)}, u32[]{:S(2)}) %all-to-all-start.1) | async-done | bytes 327712 | tf_op jit(solution)/shard_map/all_to_all | solution.py:445
  48.7 1.3 %collective-permute-start = (bf16[8,160,128]{2,1,0:T(8,128)(2,1)S(1)}, bf16[8,160,128]{2,1,0:T(8,128)(2,1)S(1)}, u32[]{:S(2)}, u32[]{:S(2)}) collective-permute-start(bf16[8,160,128]{2,1,0:T(8,128)(2,1)S(1)} %all-to-all-done.1.a_ref), channel_id=1, source_target_pairs={{0,2},{1,3},{2,0},{3,1},{4,6},{5,7},{6,4},{7,5},{8,10},{9,11},{10,... | collective-permute-start | bytes 983048 | tf_op jit(solution)/shard_map/ppermute | solution.py:366
  50.0 3.4 %collective-permute-start.4 = (bf16[8,160,128]{2,1,0:T(8,128)(2,1)S(1)}, bf16[8,160,128]{2,1,0:T(8,128)(2,1)}, u32[]{:S(2)}, u32[]{:S(2)}) collective-permute-start(bf16[8,160,128]{2,1,0:T(8,128)(2,1)S(1)} %all-to-all-done.1.a_ref), channel_id=1, source_target_pairs={{0,1},{1,0},{2,3},{3,2},{4,5},{5,4},{6,7},{7,6},{8,9},{9,8},{10,11... | collective-permute-start | bytes 983048 | tf_op jit(solution)/shard_map/ppermute | solution.py:366
  53.4 1.2 %collective-permute-done.refs_0_ = bf16[8,160,128]{2,1,0:T(8,128)(2,1)S(1)} collective-permute-done((bf16[8,160,128]{2,1,0:T(8,128)(2,1)S(1)}, bf16[8,160,128]{2,1,0:T(8,128)(2,1)S(1)}, u32[]{:S(2)}, u32[]{:S(2)}) %collective-permute-start) | collective-permute-done | bytes 327712 | tf_op jit(solution)/shard_map/ppermute | solution.py:366
  54.6 4.3 %collective-permute-start.1 = (bf16[8,160,128]{2,1,0:T(8,128)(2,1)S(1)}, bf16[8,160,128]{2,1,0:T(8,128)(2,1)}, u32[]{:S(2)}, u32[]{:S(2)}) collective-permute-start(bf16[8,160,128]{2,1,0:T(8,128)(2,1)S(1)} %collective-permute-done.refs_0_), channel_id=1, source_target_pairs={{0,1},{1,0},{2,3},{3,2},{4,5},{5,4},{6,7},{7,6},{8,9},{9,8},{10,11... | collective-permute-start | bytes 983048 | tf_op jit(solution)/shard_map/ppermute | solution.py:366
  59.2 2.8 %begin.1.refs_4_ = f32[512,1280]{1,0:T(8,128)S(1)} custom-call(bf16[8,160,128]{2,1,0:T(8,128)(2,1)S(1)} %all-to-all-done.1.a_ref, bf16[8,160,128]{2,1,0:T(8,128)(2,1)} %collective-permute-done.4.b_ref, bf16[320,1280]{1,0:T(8,128)(2,1)} %wa_ref.1, bf16[320,1280]{1,0:T(8,128)(2,1)} %collective-permute-done.5.wb_ref, bf16[64,1280]{1,0:T(8,128)(2,1)S(1)} %copy-done.8), custom_call_target="tpu_custom_call" | custom-call | tf_op jit(solution)/shard_map/begin/pallas_call | solution.py:467
  62.0 1.7 %copy-done.6 = bf16[1280,1024]{1,0:T(8,128)(2,1)S(1)} copy-done((bf16[1280,1024]{1,0:T(8,128)(2,1)S(1)}, bf16[1280,1024]{1,0:T(8,128)(2,1)}, u32[]{:S(2)}) %copy-start.6) | copy-done | bytes 2621464
  63.7 10.8 %cross.1 = (bf16[64,1280]{1,0:T(8,128)(2,1)}, bf16[512,1024]{1,0:T(8,128)(2,1)}) custom-call(s32[1]{0:T(128)} %bitcast.me_ref, bf16[8,160,128]{2,1,0:T(8,128)(2,1)S(1)} %collective-permute-done.refs_0_, bf16[8,160,128]{2,1,0:T(8,128)(2,1)} %collective-permute-done.1.refs_1_, bf16[320,1280]{1,0:T(8,128)(2,1)} %collective-permute-done.2.refs_2_, ...), custom_call_target="tpu_custom_call" | custom-call | tf_op jit(solution)/shard_map/cross/pallas_call | solution.py:482
  (30 shorter events, 0.9 us)
Async XLA Ops:
  0.6 1.1 %copy-start = (bf16[1280,320]{0,1:T(8,128)(2,1)S(1)}, bf16[1280,320]{0,1:T(8,128)(2,1)}, u32[]{:S(2)}) copy-start(bf16[1280,320]{0,1:T(8,128)(2,1)} %param.18) | copy-start | bytes 2457604
  1.8 1.1 %copy-start.2 = (bf16[1280,320]{0,1:T(8,128)(2,1)S(1)}, bf16[1280,320]{0,1:T(8,128)(2,1)}, u32[]{:S(2)}) copy-start(bf16[1280,320]{0,1:T(8,128)(2,1)} %param.19) | copy-start | bytes 2457604
  2.9 1.7 %copy-start.4 = (bf16[1024,1280]{1,0:T(8,128)(2,1)S(1)}, bf16[1024,1280]{1,0:T(8,128)(2,1)}, u32[]{:S(2)}) copy-start(bf16[1024,1280]{1,0:T(8,128)(2,1)} %patches_hbm.1) | copy-start | bytes 7864324
  4.7 0.9 %copy-start.7 = (bf16[64,1280]{1,0:T(8,128)(2,1)S(1)}, bf16[64,1280]{1,0:T(8,128)(2,1)}, u32[]{:S(2)}) copy-start(bf16[64,1280]{1,0:T(8,128)(2,1)} %init_ref.1) | copy-start | bytes 491524
  5.6 1.1 %copy-start.10 = (bf16[1280,320]{0,1:T(8,128)(2,1)S(1)}, bf16[1280,320]{0,1:T(8,128)(2,1)}, u32[]{:S(2)}) copy-start(bf16[1280,320]{0,1:T(8,128)(2,1)} %param.17) | copy-start | bytes 2457604
  6.7 0.7 copy-start.11
  7.4 0.7 copy-start.12
  8.1 18.0 %copy-start.1 = (bf16[1280,320]{0,1:T(8,128)(2,1)S(1)}, bf16[1280,320]{0,1:T(8,128)(2,1)}, u32[]{:S(2)}) copy-start(bf16[1280,320]{0,1:T(8,128)(2,1)} %param.18) | copy-start | bytes 2457604
  8.1 18.0 %copy-start.3 = (bf16[1280,320]{0,1:T(8,128)(2,1)S(1)}, bf16[1280,320]{0,1:T(8,128)(2,1)}, u32[]{:S(2)}) copy-start(bf16[1280,320]{0,1:T(8,128)(2,1)} %param.19) | copy-start | bytes 2457604
  8.1 18.0 %copy-start.8 = (bf16[64,1280]{1,0:T(8,128)(2,1)S(1)}, bf16[64,1280]{1,0:T(8,128)(2,1)}, u32[]{:S(2)}) copy-start(bf16[64,1280]{1,0:T(8,128)(2,1)} %init_ref.1) | copy-start | bytes 491524
  18.5 40.5 %copy-start.13 = (s32[8]{0:T(128)S(1)}, s32[8]{0:T(128)}, u32[]{:S(2)}) copy-start(s32[8]{0:T(128)} %owner_ref.1) | copy-start | bytes 100
  18.5 40.4 %copy-start.14 = (s32[32,4]{0,1:T(4,128)S(1)}, s32[32,4]{0,1:T(4,128)}, u32[]{:S(2)}) copy-start(s32[32,4]{0,1:T(4,128)} %param.15) | copy-start | bytes 1540
  18.5 15.1 %all-to-all-start = ((bf16[8,176,128]{2,1,0:T(8,128)(2,1)}), bf16[8,176,128]{2,1,0:T(8,128)(2,1)S(1)}, u32[]{:S(2)}, u32[]{:S(2)}) async-start(bf16[8,176,128]{2,1,0:T(8,128)(2,1)} %get-tuple-element.4), calls=%async_computation | async-start | bytes 720896 | tf_op jit(solution)/shard_map/all_to_all | solution.py:425
  24.9 19.2 %collective-permute-start.2 = (bf16[320,1280]{1,0:T(8,128)(2,1)}, bf16[320,1280]{1,0:T(8,128)(2,1)}, u32[]{:S(2)}, u32[]{:S(2)}) collective-permute-start(bf16[320,1280]{1,0:T(8,128)(2,1)} %wa_ref.1), channel_id=1, source_target_pairs={{0,2},{1,3},{2,0},{3,1},{4,6},{5,7},{6,4},{7,5},{8,10},{9,11},{10,... | collective-permute-start | bytes 2457608 | tf_op jit(solution)/shard_map/ppermute | solution.py:366
  34.9 13.8 %all-to-all-start.1 = ((bf16[8,160,128]{2,1,0:T(8,128)(2,1)}), bf16[8,160,128]{2,1,0:T(8,128)(2,1)S(1)}, u32[]{:S(2)}, u32[]{:S(2)}) async-start(bf16[8,160,128]{2,1,0:T(8,128)(2,1)} %merge.1), calls=%async_computation.1 | async-start | bytes 655360 | tf_op jit(solution)/shard_map/all_to_all | solution.py:445
  40.6 21.4 %copy-start.5 = (bf16[1280,1024]{1,0:T(8,128)(2,1)S(1)}, bf16[1280,1024]{1,0:T(8,128)(2,1)}, u32[]{:S(2)}) copy-start(bf16[1280,1024]{1,0:T(8,128)(2,1)} %refs_7_.1) | copy-start | bytes 7864324
  40.6 18.6 %collective-permute-start.5 = (bf16[320,1280]{1,0:T(8,128)(2,1)}, bf16[320,1280]{1,0:T(8,128)(2,1)}, u32[]{:S(2)}, u32[]{:S(2)}) collective-permute-start(bf16[320,1280]{1,0:T(8,128)(2,1)} %wa_ref.1), channel_id=1, source_target_pairs={{0,1},{1,0},{2,3},{3,2},{4,5},{5,4},{6,7},{7,6},{8,9},{9,8},{10,11... | collective-permute-start | bytes 2457608 | tf_op jit(solution)/shard_map/ppermute | solution.py:366
  44.0 17.9 %collective-permute-start.3 = (bf16[320,1280]{1,0:T(8,128)(2,1)}, bf16[320,1280]{1,0:T(8,128)(2,1)}, u32[]{:S(2)}, u32[]{:S(2)}) collective-permute-start(bf16[320,1280]{1,0:T(8,128)(2,1)} %collective-permute-done.2.refs_2_), channel_id=1, source_target_pairs={{0,1},{1,0},{2,3},{3,2},{4,5},{5,4},{6,7},{7,6},{8,9},{9,8},{10,11... | collective-permute-start | bytes 2457608 | tf_op jit(solution)/shard_map/ppermute | solution.py:366
  48.7 5.9 %collective-permute-start = (bf16[8,160,128]{2,1,0:T(8,128)(2,1)S(1)}, bf16[8,160,128]{2,1,0:T(8,128)(2,1)S(1)}, u32[]{:S(2)}, u32[]{:S(2)}) collective-permute-start(bf16[8,160,128]{2,1,0:T(8,128)(2,1)S(1)} %all-to-all-done.1.a_ref), channel_id=1, source_target_pairs={{0,2},{1,3},{2,0},{3,1},{4,6},{5,7},{6,4},{7,5},{8,10},{9,11},{10,... | collective-permute-start | bytes 983048 | tf_op jit(solution)/shard_map/ppermute | solution.py:366
  50.0 9.2 %collective-permute-start.4 = (bf16[8,160,128]{2,1,0:T(8,128)(2,1)S(1)}, bf16[8,160,128]{2,1,0:T(8,128)(2,1)}, u32[]{:S(2)}, u32[]{:S(2)}) collective-permute-start(bf16[8,160,128]{2,1,0:T(8,128)(2,1)S(1)} %all-to-all-done.1.a_ref), channel_id=1, source_target_pairs={{0,1},{1,0},{2,3},{3,2},{4,5},{5,4},{6,7},{7,6},{8,9},{9,8},{10,11... | collective-permute-start | bytes 983048 | tf_op jit(solution)/shard_map/ppermute | solution.py:366
  54.6 7.3 %collective-permute-start.1 = (bf16[8,160,128]{2,1,0:T(8,128)(2,1)S(1)}, bf16[8,160,128]{2,1,0:T(8,128)(2,1)}, u32[]{:S(2)}, u32[]{:S(2)}) collective-permute-start(bf16[8,160,128]{2,1,0:T(8,128)(2,1)S(1)} %collective-permute-done.refs_0_), channel_id=1, source_target_pairs={{0,1},{1,0},{2,3},{3,2},{4,5},{5,4},{6,7},{7,6},{8,9},{9,8},{10,11... | collective-permute-start | bytes 983048 | tf_op jit(solution)/shard_map/ppermute | solution.py:366
  59.1 2.8 %copy-start.9 = (bf16[512,1024]{1,0:T(8,128)(2,1)S(1)}, bf16[512,1024]{1,0:T(8,128)(2,1)}, u32[]{:S(2)}) copy-start(bf16[512,1024]{1,0:T(8,128)(2,1)} %refs_6_.1) | copy-start | bytes 3145732
  62.0 1.7 %copy-start.6 = (bf16[1280,1024]{1,0:T(8,128)(2,1)S(1)}, bf16[1280,1024]{1,0:T(8,128)(2,1)}, u32[]{:S(2)}) copy-start(bf16[1280,1024]{1,0:T(8,128)(2,1)} %refs_8_.1) | copy-start | bytes 7864324
